TPU v7x, 128 devices: a whole 4x4x4 slice. The times are simulated.
128 devices in a mesh: seq: 32 (over z, x, core), head: 4 (over y).
Axes of the slice: x: 4, y: 4, z: 4, core: 2. Of those that a mesh axis runs over, the one named last changes fastest.
Arguments:
- hidden: bfloat16 [8192, 2048], P('seq'), may hold values from -6 to 6
- w_query: bfloat16 [2048, 2048], P(None, 'head'), may hold values from -0.125 to 0.125
- w_key: bfloat16 [2048, 2048], P(None, 'head'), as said below
- w_value: bfloat16 [2048, 4096], P(None, 'head'), may hold values from -0.125 to 0.125
- w_gate: bfloat16 [2048, 4096], P(None, 'head'), may hold values from -0.125 to 0.125
- w_beta: bfloat16 [2048, 32], P(None, 'head'), may hold values from -0.125 to 0.125
- conv_query: bfloat16 [4, 2048], P(None, 'head'), may hold values from -3 to 3
- conv_key: bfloat16 [4, 2048], P(None, 'head'), may hold values from -3 to 3
- conv_value: bfloat16 [4, 4096], P(None, 'head'), may hold values from -3 to 3
- norm_gain: bfloat16 [128], replicated, may hold values from 0.5 to 1.5
- w_out: bfloat16 [4096, 2048], P('head'), may hold values from -0.09375 to 0.09375
Outputs:
- mixed: bfloat16 [8192, 2048], P('seq', 'head')
Inputs may be any that keep to these rules, and one draw needn't show every extreme that they name: `w_key`: entries of the key projection.
All inputs are finite; a program needn't handle non-finite values.
Results may differ from a plain program's by a relative error of at most 0.017.
Values may be sent and summed in bfloat16 or wider, within the bound.
A program may use at most 128 MiB of HBM per device.

v0:
```python
import jax
import jax.numpy as jnp
from jax import lax
from jax.sharding import PartitionSpec as P

DK = 128
DV = 128
KER = 4
SPAN = 64


exact_mode = lax.Precision.HIGHEST
eps_norm = 1e-06


def from_behind(block, axis, distance):
    devices = range(lax.axis_size(axis))
    route = [(i - distance, i) for i in devices if i - distance in devices]
    return lax.ppermute(block, axis, route)


def contract(form, left, right):
    return jnp.einsum(form, left, right, precision=exact_mode)


def unit_rows(values):
    return values * lax.rsqrt(jnp.sum(values * values, axis=-1, keepdims=True) + eps_norm)


def convolve(projected, rim_rows, kernel):
    padded = jnp.concatenate([rim_rows, projected], axis=0).astype(jnp.float32)
    count_rows = projected.shape[0]
    summed = jnp.zeros((count_rows, projected.shape[1]), jnp.float32)
    for offset in range(KER):
        summed = summed + kernel[offset].astype(jnp.float32) * padded[offset : offset + count_rows]
    return jax.nn.silu(summed)


def delta_block(state_now, inputs):
    queries, key_act, values, beta_gate = inputs
    size_block = key_act.shape[1]
    key_gram = contract("hcd,hed->hce", key_act, key_act)
    below = jnp.tril(jnp.ones((size_block, size_block), jnp.float32), -1)
    unit_diag = jnp.eye(size_block, dtype=jnp.float32)
    system = unit_diag + beta_gate[:, :, None] * key_gram * below
    solved_keys = lax.linalg.triangular_solve(
        system, beta_gate[:, :, None] * key_act, left_side=True, lower=True
    )
    solved_values = lax.linalg.triangular_solve(
        system, beta_gate[:, :, None] * values, left_side=True, lower=True
    )
    updates = solved_values - contract("hcd,hvd->hcv", solved_keys, state_now)
    attend = contract("hcd,hed->hce", queries, key_act) * (below + unit_diag)
    outputs = contract("hcd,hvd->hcv", queries, state_now) + contract(
        "hce,hev->hcv", attend, updates
    )
    state_next = state_now + contract("hcv,hcd->hvd", updates, key_act)
    return (state_next, outputs)


def delta_pass(queries, key_act, values, beta_gate, state_start):
    count_rows = queries.shape[0]
    blocks = count_rows // SPAN

    def arrange(array):
        return jnp.moveaxis(array.reshape((blocks, SPAN) + array.shape[1:]), 1, 2)

    return lax.scan(
        delta_block,
        state_start,
        (arrange(queries), arrange(key_act), arrange(values), arrange(beta_gate)),
    )


def shards(
    hidden,
    w_query,
    w_key,
    w_value,
    w_gate,
    w_beta,
    conv_query,
    conv_key,
    conv_value,
    norm_gain,
    w_out,
):
    count_rows = hidden.shape[0]
    heads_key = w_query.shape[1] // DK
    heads_value = w_value.shape[1] // DV
    q_proj = jnp.dot(hidden, w_query, preferred_element_type=jnp.float32).astype(jnp.bfloat16)
    k_proj = jnp.dot(hidden, w_key, preferred_element_type=jnp.float32).astype(jnp.bfloat16)
    v_proj = jnp.dot(hidden, w_value, preferred_element_type=jnp.float32).astype(jnp.bfloat16)
    gate_proj = jnp.dot(hidden, w_gate, preferred_element_type=jnp.float32).astype(jnp.bfloat16)
    beta_gate = 0.05 + 0.15 * jax.nn.sigmoid(
        jnp.dot(hidden, w_beta, preferred_element_type=jnp.float32)
    )
    rim_count = KER - 1
    rim_sets = from_behind(
        (
            q_proj[count_rows - rim_count :],
            k_proj[count_rows - rim_count :],
            v_proj[count_rows - rim_count :],
        ),
        "seq",
        1,
    )
    queries = unit_rows(
        convolve(q_proj, rim_sets[0], conv_query).reshape(count_rows, heads_key, DK)
    )
    key_act = unit_rows(convolve(k_proj, rim_sets[1], conv_key).reshape(count_rows, heads_key, DK))
    values = convolve(v_proj, rim_sets[2], conv_value).reshape(count_rows, heads_value, DV)
    group_size = heads_value // heads_key
    queries = jnp.repeat(queries, group_size, axis=1)
    key_act = jnp.repeat(key_act, group_size, axis=1)
    extended = jnp.concatenate(
        [values, jnp.zeros((count_rows, heads_value, DK), jnp.float32)], axis=2
    )
    identity_block = jnp.broadcast_to(jnp.eye(DK, dtype=jnp.float32), (heads_value, DK, DK))
    empty_state = jnp.zeros((heads_value, DV, DK), jnp.float32)
    state_end, outputs = delta_pass(
        queries,
        key_act,
        extended,
        beta_gate,
        jnp.concatenate([empty_state, identity_block], axis=1),
    )
    local_state = state_end[:, :DV]
    transit = state_end[:, DV:]

    def advance(step_index, incoming_state):
        outgoing = contract("hvd,hde->hve", incoming_state, transit) + local_state
        return from_behind(outgoing.astype(jnp.bfloat16), "seq", 1).astype(outgoing.dtype)

    incoming_state = lax.fori_loop(0, lax.axis_size("seq") - 1, advance, empty_state)
    block_out = outputs[..., :DV] + contract("nhcd,hvd->nhcv", outputs[..., DV:], incoming_state)
    attended = jnp.moveaxis(block_out, 2, 1).reshape(count_rows, heads_value, DV)
    scale_rms = lax.rsqrt(jnp.mean(attended * attended, axis=-1, keepdims=True) + eps_norm)
    gate_act = jax.nn.silu(gate_proj.astype(jnp.float32).reshape(count_rows, heads_value, DV))
    normed = attended * scale_rms * norm_gain.astype(jnp.float32) * gate_act
    gated = normed.reshape(count_rows, heads_value * DV).astype(jnp.bfloat16)
    partial_sum = jnp.dot(gated, w_out, preferred_element_type=jnp.float32)
    rounded = lax.optimization_barrier(partial_sum.astype(jnp.bfloat16)).astype(jnp.float32)
    mixed = lax.psum_scatter(rounded.astype(jnp.bfloat16), "head", scatter_dimension=1, tiled=True)
    return mixed


def solution(mesh):
    in_specs = (
        P("seq", None),
        P(None, "head"),
        P(None, "head"),
        P(None, "head"),
        P(None, "head"),
        P(None, "head"),
        P(None, "head"),
        P(None, "head"),
        P(None, "head"),
        P(),
        P("head", None),
    )
    out_specs = P("seq", "head")
    return jax.shard_map(shards, mesh=mesh, in_specs=in_specs, out_specs=out_specs, check_vma=False)
```

profile of v0, /device:TPU:64, one launch (start us, length us, event | category | flops | bytes accessed | tf_op | source)
XLA Modules:
  0.0 683.2 jit_solution(556424875188565715)
XLA Ops:
  12.2 2.3 convolution_convert_fusion.3
  14.6 3.6 collective-permute-start.3
  27.9 2.2 broadcast_multiply_fusion.1
  40.9 206.7 %while.23 = (s32[]{:T(128)}, f32[8,256,128]{2,1,0:T(8,128)S(1)}, f32[4,8,64,256]{3,2,0,1:T(8,128)}, f32[4,8,64]{2,1,0:T(8,128)S(1)}, f32[4,8,64,128]{3,2,0,1:T(8...) while((s32[]{:T(128)}, f32[8,256,128]{2,1,0:T(8,128)S(1)}, ...), condition=%wide.region_3.4_spmd, body=%wide.region_2.3_spmd.sunk | while | flops 957218880 | bytes 21372060 | solution.py:68
  41.0 2.3 fusion.124
  43.3 40.0 %custom-call.8 = f32[8,1,64,64]{2,3,1,0:T(8,128)S(1)} custom-call(f32[8,1,64,64]{3,2,1,0:T(8,128)} %fusion.124), custom_call_target="InvertDiagBlocksLowerTriangular" | custom-call | tf_op jit(solution)/shard_map/while/body/eval_jaxpr/triangular_solve | solution.py:49
  92.6 2.3 fusion.124
  94.9 40.0 %custom-call.8 = f32[8,1,64,64]{2,3,1,0:T(8,128)S(1)} custom-call(f32[8,1,64,64]{3,2,1,0:T(8,128)} %fusion.124), custom_call_target="InvertDiagBlocksLowerTriangular" | custom-call | tf_op jit(solution)/shard_map/while/body/eval_jaxpr/triangular_solve | solution.py:49
  144.3 2.3 fusion.124
  146.6 40.0 %custom-call.8 = f32[8,1,64,64]{2,3,1,0:T(8,128)S(1)} custom-call(f32[8,1,64,64]{3,2,1,0:T(8,128)} %fusion.124), custom_call_target="InvertDiagBlocksLowerTriangular" | custom-call | tf_op jit(solution)/shard_map/while/body/eval_jaxpr/triangular_solve | solution.py:49
  196.0 2.3 fusion.124
  198.3 40.0 %custom-call.8 = f32[8,1,64,64]{2,3,1,0:T(8,128)S(1)} custom-call(f32[8,1,64,64]{3,2,1,0:T(8,128)} %fusion.124), custom_call_target="InvertDiagBlocksLowerTriangular" | custom-call | tf_op jit(solution)/shard_map/while/body/eval_jaxpr/triangular_solve | solution.py:49
  248.6 392.0 %while.24 = (s32[]{:T(128)}, f32[8,128,128]{2,1,0:T(8,128)}, f32[8,128,128]{2,1,0:T(8,128)}, f32[8,128,128]{2,1,0:T(8,128)}, s32[]{:T(128)}, /*index=5*/s32[]{:T(128)}) while((s32[]{:T(128)}, f32[8,128,128]{2,1,0:T(8,128)}, f32[8,128,128]{2,1,0:T(8,128)}, f32[8,128,128]{2,1,0:T(8,128)}, s32[]{:T(128)}, /*index=5*/s32[]{:T(128)}) %tuple.57), condition=%wide.region_5.6_spmd.clone, body=%wide.region_4.5_spmd.clone.sunk | while | flops 201850880 | bytes 3670135 | solution.py:135
  250.5 3.5 collective-permute-start
  254.0 6.3 collective-permute-done
  265.1 7.9 %collective-permute-done = bf16[8,128,128]{2,1,0:T(8,128)(2,1)S(1)} collective-permute-done((bf16[8,128,128]{2,1,0:T(8,128)(2,1)S(1)}, bf16[8,128,128]{2,1,0:T(8,128)(2,1)S(1)}, u32[]{:S(2)}, u32[]{:S(2)}) %collective-permute-start) | collective-permute-done | bytes 262176 | tf_op jit(solution)/shard_map/while/body/eval_jaxpr/ppermute | solution.py:19
  277.7 7.9 %collective-permute-done = bf16[8,128,128]{2,1,0:T(8,128)(2,1)S(1)} collective-permute-done((bf16[8,128,128]{2,1,0:T(8,128)(2,1)S(1)}, bf16[8,128,128]{2,1,0:T(8,128)(2,1)S(1)}, u32[]{:S(2)}, u32[]{:S(2)}) %collective-permute-start) | collective-permute-done | bytes 262176 | tf_op jit(solution)/shard_map/while/body/eval_jaxpr/ppermute | solution.py:19
  290.4 7.9 %collective-permute-done = bf16[8,128,128]{2,1,0:T(8,128)(2,1)S(1)} collective-permute-done((bf16[8,128,128]{2,1,0:T(8,128)(2,1)S(1)}, bf16[8,128,128]{2,1,0:T(8,128)(2,1)S(1)}, u32[]{:S(2)}, u32[]{:S(2)}) %collective-permute-start) | collective-permute-done | bytes 262176 | tf_op jit(solution)/shard_map/while/body/eval_jaxpr/ppermute | solution.py:19
  303.0 7.9 %collective-permute-done = bf16[8,128,128]{2,1,0:T(8,128)(2,1)S(1)} collective-permute-done((bf16[8,128,128]{2,1,0:T(8,128)(2,1)S(1)}, bf16[8,128,128]{2,1,0:T(8,128)(2,1)S(1)}, u32[]{:S(2)}, u32[]{:S(2)}) %collective-permute-start) | collective-permute-done | bytes 262176 | tf_op jit(solution)/shard_map/while/body/eval_jaxpr/ppermute | solution.py:19
  315.7 7.9 %collective-permute-done = bf16[8,128,128]{2,1,0:T(8,128)(2,1)S(1)} collective-permute-done((bf16[8,128,128]{2,1,0:T(8,128)(2,1)S(1)}, bf16[8,128,128]{2,1,0:T(8,128)(2,1)S(1)}, u32[]{:S(2)}, u32[]{:S(2)}) %collective-permute-start) | collective-permute-done | bytes 262176 | tf_op jit(solution)/shard_map/while/body/eval_jaxpr/ppermute | solution.py:19
  328.3 7.9 %collective-permute-done = bf16[8,128,128]{2,1,0:T(8,128)(2,1)S(1)} collective-permute-done((bf16[8,128,128]{2,1,0:T(8,128)(2,1)S(1)}, bf16[8,128,128]{2,1,0:T(8,128)(2,1)S(1)}, u32[]{:S(2)}, u32[]{:S(2)}) %collective-permute-start) | collective-permute-done | bytes 262176 | tf_op jit(solution)/shard_map/while/body/eval_jaxpr/ppermute | solution.py:19
  341.0 7.9 %collective-permute-done = bf16[8,128,128]{2,1,0:T(8,128)(2,1)S(1)} collective-permute-done((bf16[8,128,128]{2,1,0:T(8,128)(2,1)S(1)}, bf16[8,128,128]{2,1,0:T(8,128)(2,1)S(1)}, u32[]{:S(2)}, u32[]{:S(2)}) %collective-permute-start) | collective-permute-done | bytes 262176 | tf_op jit(solution)/shard_map/while/body/eval_jaxpr/ppermute | solution.py:19
  353.6 7.9 %collective-permute-done = bf16[8,128,128]{2,1,0:T(8,128)(2,1)S(1)} collective-permute-done((bf16[8,128,128]{2,1,0:T(8,128)(2,1)S(1)}, bf16[8,128,128]{2,1,0:T(8,128)(2,1)S(1)}, u32[]{:S(2)}, u32[]{:S(2)}) %collective-permute-start) | collective-permute-done | bytes 262176 | tf_op jit(solution)/shard_map/while/body/eval_jaxpr/ppermute | solution.py:19
  366.3 7.9 %collective-permute-done = bf16[8,128,128]{2,1,0:T(8,128)(2,1)S(1)} collective-permute-done((bf16[8,128,128]{2,1,0:T(8,128)(2,1)S(1)}, bf16[8,128,128]{2,1,0:T(8,128)(2,1)S(1)}, u32[]{:S(2)}, u32[]{:S(2)}) %collective-permute-start) | collective-permute-done | bytes 262176 | tf_op jit(solution)/shard_map/while/body/eval_jaxpr/ppermute | solution.py:19
  378.9 7.9 %collective-permute-done = bf16[8,128,128]{2,1,0:T(8,128)(2,1)S(1)} collective-permute-done((bf16[8,128,128]{2,1,0:T(8,128)(2,1)S(1)}, bf16[8,128,128]{2,1,0:T(8,128)(2,1)S(1)}, u32[]{:S(2)}, u32[]{:S(2)}) %collective-permute-start) | collective-permute-done | bytes 262176 | tf_op jit(solution)/shard_map/while/body/eval_jaxpr/ppermute | solution.py:19
  391.5 7.9 %collective-permute-done = bf16[8,128,128]{2,1,0:T(8,128)(2,1)S(1)} collective-permute-done((bf16[8,128,128]{2,1,0:T(8,128)(2,1)S(1)}, bf16[8,128,128]{2,1,0:T(8,128)(2,1)S(1)}, u32[]{:S(2)}, u32[]{:S(2)}) %collective-permute-start) | collective-permute-done | bytes 262176 | tf_op jit(solution)/shard_map/while/body/eval_jaxpr/ppermute | solution.py:19
  404.2 7.9 %collective-permute-done = bf16[8,128,128]{2,1,0:T(8,128)(2,1)S(1)} collective-permute-done((bf16[8,128,128]{2,1,0:T(8,128)(2,1)S(1)}, bf16[8,128,128]{2,1,0:T(8,128)(2,1)S(1)}, u32[]{:S(2)}, u32[]{:S(2)}) %collective-permute-start) | collective-permute-done | bytes 262176 | tf_op jit(solution)/shard_map/while/body/eval_jaxpr/ppermute | solution.py:19
  416.8 7.9 %collective-permute-done = bf16[8,128,128]{2,1,0:T(8,128)(2,1)S(1)} collective-permute-done((bf16[8,128,128]{2,1,0:T(8,128)(2,1)S(1)}, bf16[8,128,128]{2,1,0:T(8,128)(2,1)S(1)}, u32[]{:S(2)}, u32[]{:S(2)}) %collective-permute-start) | collective-permute-done | bytes 262176 | tf_op jit(solution)/shard_map/while/body/eval_jaxpr/ppermute | solution.py:19
  429.5 7.9 %collective-permute-done = bf16[8,128,128]{2,1,0:T(8,128)(2,1)S(1)} collective-permute-done((bf16[8,128,128]{2,1,0:T(8,128)(2,1)S(1)}, bf16[8,128,128]{2,1,0:T(8,128)(2,1)S(1)}, u32[]{:S(2)}, u32[]{:S(2)}) %collective-permute-start) | collective-permute-done | bytes 262176 | tf_op jit(solution)/shard_map/while/body/eval_jaxpr/ppermute | solution.py:19
  442.1 7.9 %collective-permute-done = bf16[8,128,128]{2,1,0:T(8,128)(2,1)S(1)} collective-permute-done((bf16[8,128,128]{2,1,0:T(8,128)(2,1)S(1)}, bf16[8,128,128]{2,1,0:T(8,128)(2,1)S(1)}, u32[]{:S(2)}, u32[]{:S(2)}) %collective-permute-start) | collective-permute-done | bytes 262176 | tf_op jit(solution)/shard_map/while/body/eval_jaxpr/ppermute | solution.py:19
  454.8 7.9 %collective-permute-done = bf16[8,128,128]{2,1,0:T(8,128)(2,1)S(1)} collective-permute-done((bf16[8,128,128]{2,1,0:T(8,128)(2,1)S(1)}, bf16[8,128,128]{2,1,0:T(8,128)(2,1)S(1)}, u32[]{:S(2)}, u32[]{:S(2)}) %collective-permute-start) | collective-permute-done | bytes 262176 | tf_op jit(solution)/shard_map/while/body/eval_jaxpr/ppermute | solution.py:19
  467.4 7.9 %collective-permute-done = bf16[8,128,128]{2,1,0:T(8,128)(2,1)S(1)} collective-permute-done((bf16[8,128,128]{2,1,0:T(8,128)(2,1)S(1)}, bf16[8,128,128]{2,1,0:T(8,128)(2,1)S(1)}, u32[]{:S(2)}, u32[]{:S(2)}) %collective-permute-start) | collective-permute-done | bytes 262176 | tf_op jit(solution)/shard_map/while/body/eval_jaxpr/ppermute | solution.py:19
  480.1 7.9 %collective-permute-done = bf16[8,128,128]{2,1,0:T(8,128)(2,1)S(1)} collective-permute-done((bf16[8,128,128]{2,1,0:T(8,128)(2,1)S(1)}, bf16[8,128,128]{2,1,0:T(8,128)(2,1)S(1)}, u32[]{:S(2)}, u32[]{:S(2)}) %collective-permute-start) | collective-permute-done | bytes 262176 | tf_op jit(solution)/shard_map/while/body/eval_jaxpr/ppermute | solution.py:19
  492.7 7.9 %collective-permute-done = bf16[8,128,128]{2,1,0:T(8,128)(2,1)S(1)} collective-permute-done((bf16[8,128,128]{2,1,0:T(8,128)(2,1)S(1)}, bf16[8,128,128]{2,1,0:T(8,128)(2,1)S(1)}, u32[]{:S(2)}, u32[]{:S(2)}) %collective-permute-start) | collective-permute-done | bytes 262176 | tf_op jit(solution)/shard_map/while/body/eval_jaxpr/ppermute | solution.py:19
  505.4 7.9 %collective-permute-done = bf16[8,128,128]{2,1,0:T(8,128)(2,1)S(1)} collective-permute-done((bf16[8,128,128]{2,1,0:T(8,128)(2,1)S(1)}, bf16[8,128,128]{2,1,0:T(8,128)(2,1)S(1)}, u32[]{:S(2)}, u32[]{:S(2)}) %collective-permute-start) | collective-permute-done | bytes 262176 | tf_op jit(solution)/shard_map/while/body/eval_jaxpr/ppermute | solution.py:19
  518.0 7.9 %collective-permute-done = bf16[8,128,128]{2,1,0:T(8,128)(2,1)S(1)} collective-permute-done((bf16[8,128,128]{2,1,0:T(8,128)(2,1)S(1)}, bf16[8,128,128]{2,1,0:T(8,128)(2,1)S(1)}, u32[]{:S(2)}, u32[]{:S(2)}) %collective-permute-start) | collective-permute-done | bytes 262176 | tf_op jit(solution)/shard_map/while/body/eval_jaxpr/ppermute | solution.py:19
  530.7 7.9 %collective-permute-done = bf16[8,128,128]{2,1,0:T(8,128)(2,1)S(1)} collective-permute-done((bf16[8,128,128]{2,1,0:T(8,128)(2,1)S(1)}, bf16[8,128,128]{2,1,0:T(8,128)(2,1)S(1)}, u32[]{:S(2)}, u32[]{:S(2)}) %collective-permute-start) | collective-permute-done | bytes 262176 | tf_op jit(solution)/shard_map/while/body/eval_jaxpr/ppermute | solution.py:19
  543.3 7.9 %collective-permute-done = bf16[8,128,128]{2,1,0:T(8,128)(2,1)S(1)} collective-permute-done((bf16[8,128,128]{2,1,0:T(8,128)(2,1)S(1)}, bf16[8,128,128]{2,1,0:T(8,128)(2,1)S(1)}, u32[]{:S(2)}, u32[]{:S(2)}) %collective-permute-start) | collective-permute-done | bytes 262176 | tf_op jit(solution)/shard_map/while/body/eval_jaxpr/ppermute | solution.py:19
  556.0 7.9 %collective-permute-done = bf16[8,128,128]{2,1,0:T(8,128)(2,1)S(1)} collective-permute-done((bf16[8,128,128]{2,1,0:T(8,128)(2,1)S(1)}, bf16[8,128,128]{2,1,0:T(8,128)(2,1)S(1)}, u32[]{:S(2)}, u32[]{:S(2)}) %collective-permute-start) | collective-permute-done | bytes 262176 | tf_op jit(solution)/shard_map/while/body/eval_jaxpr/ppermute | solution.py:19
  568.6 7.9 %collective-permute-done = bf16[8,128,128]{2,1,0:T(8,128)(2,1)S(1)} collective-permute-done((bf16[8,128,128]{2,1,0:T(8,128)(2,1)S(1)}, bf16[8,128,128]{2,1,0:T(8,128)(2,1)S(1)}, u32[]{:S(2)}, u32[]{:S(2)}) %collective-permute-start) | collective-permute-done | bytes 262176 | tf_op jit(solution)/shard_map/while/body/eval_jaxpr/ppermute | solution.py:19
  581.3 7.9 %collective-permute-done = bf16[8,128,128]{2,1,0:T(8,128)(2,1)S(1)} collective-permute-done((bf16[8,128,128]{2,1,0:T(8,128)(2,1)S(1)}, bf16[8,128,128]{2,1,0:T(8,128)(2,1)S(1)}, u32[]{:S(2)}, u32[]{:S(2)}) %collective-permute-start) | collective-permute-done | bytes 262176 | tf_op jit(solution)/shard_map/while/body/eval_jaxpr/ppermute | solution.py:19
  593.9 7.9 %collective-permute-done = bf16[8,128,128]{2,1,0:T(8,128)(2,1)S(1)} collective-permute-done((bf16[8,128,128]{2,1,0:T(8,128)(2,1)S(1)}, bf16[8,128,128]{2,1,0:T(8,128)(2,1)S(1)}, u32[]{:S(2)}, u32[]{:S(2)}) %collective-permute-start) | collective-permute-done | bytes 262176 | tf_op jit(solution)/shard_map/while/body/eval_jaxpr/ppermute | solution.py:19
  606.6 7.9 %collective-permute-done = bf16[8,128,128]{2,1,0:T(8,128)(2,1)S(1)} collective-permute-done((bf16[8,128,128]{2,1,0:T(8,128)(2,1)S(1)}, bf16[8,128,128]{2,1,0:T(8,128)(2,1)S(1)}, u32[]{:S(2)}, u32[]{:S(2)}) %collective-permute-start) | collective-permute-done | bytes 262176 | tf_op jit(solution)/shard_map/while/body/eval_jaxpr/ppermute | solution.py:19
  619.2 7.9 %collective-permute-done = bf16[8,128,128]{2,1,0:T(8,128)(2,1)S(1)} collective-permute-done((bf16[8,128,128]{2,1,0:T(8,128)(2,1)S(1)}, bf16[8,128,128]{2,1,0:T(8,128)(2,1)S(1)}, u32[]{:S(2)}, u32[]{:S(2)}) %collective-permute-start) | collective-permute-done | bytes 262176 | tf_op jit(solution)/shard_map/while/body/eval_jaxpr/ppermute | solution.py:19
  631.9 7.9 %collective-permute-done = bf16[8,128,128]{2,1,0:T(8,128)(2,1)S(1)} collective-permute-done((bf16[8,128,128]{2,1,0:T(8,128)(2,1)S(1)}, bf16[8,128,128]{2,1,0:T(8,128)(2,1)S(1)}, u32[]{:S(2)}, u32[]{:S(2)}) %collective-permute-start) | collective-permute-done | bytes 262176 | tf_op jit(solution)/shard_map/while/body/eval_jaxpr/ppermute | solution.py:19
  640.6 2.9 multiply_reduce_fusion
  645.6 7.8 %convolution_convert_fusion = bf16[256,2048]{1,0:T(8,128)(2,1)} fusion(bf16[1024,2048]{1,0:T(8,128)(2,1)} %param.25, bf16[256,2048]{1,0:T(8,128)(2,1)} %param.15, bf16[2048,1024]{1,0:T(8,128)(2,1)} %param.19, f32[32,8,8,128]{3,2,1,0:T(8,128)S(1)} %bitcast.160, f32[32,8,8,128]{3,2,1,0:T(8,128)} %bitcast.161, f32[1024]{0:T(1024)S(1)} %broadcast_bitcast_fusion), kind=kOutput, calls=%fused_computation.51 | convolution fusion | flops 2150629376 | bytes 12587008 | tf_op jit(solution)/shard_map/dot_general | solution.py:142
  653.4 22.9 %reduce-scatter.2.cloned.1.call-done = bf16[256,512]{1,0:T(8,128)(2,1)} async-done(((bf16[256,2048]{1,0:T(8,128)(2,1)}), bf16[256,512]{1,0:T(8,128)(2,1)}) %reduce-scatter.2.cloned.1.call-update) | async-done | bytes 262160 | tf_op jit(solution)/shard_map/reduce_scatter | solution.py:144
  (229 shorter events, 211.3 us)
Async XLA Ops:
  6.5 5.6 copy-start.4
  6.5 669.8 %reduce-scatter.2.cloned.1.call-start = ((), (), s32[]{:S(2)}) async-start(), calls=%async_computation.1 | async-start | bytes 1310720 | tf_op jit(solution)/shard_map/reduce_scatter | solution.py:144
  8.1 10.1 %copy-start.12 = (bf16[2048,1024]{1,0:T(8,128)(2,1)S(1)}, bf16[2048,1024]{1,0:T(8,128)(2,1)}, u32[]{:S(2)}) copy-start(bf16[2048,1024]{1,0:T(8,128)(2,1)} %param.18) | copy-start | bytes 12582916
  10.2 4.3 copy-start.7
  10.2 12.0 %collective-permute-start.1 = (bf16[3,512]{1,0:T(4,128)(2,1)S(1)}, bf16[3,512]{1,0:T(4,128)(2,1)S(1)}, u32[]{:S(2)}, u32[]{:S(2)}) collective-permute-start(bf16[3,512]{1,0:T(4,128)(2,1)S(1)} %slice.132), channel_id=1, source_target_pairs={{0,4},{4,8},{8,12},{12,16},{16,20},{20,24},{24,28},{28,32},{32,36}... | collective-permute-start | bytes 9224 | tf_op jit(solution)/shard_map/ppermute | solution.py:19
  14.5 7.0 %copy-start.10 = (bf16[4,512]{1,0:T(4,128)(2,1)S(1)}, bf16[4,512]{1,0:T(4,128)(2,1)}, u32[]{:S(2)}) copy-start(bf16[4,512]{1,0:T(4,128)(2,1)} %param.22) | copy-start | bytes 12292
  14.5 7.0 %copy-start.11 = (bf16[4,512]{1,0:T(4,128)(2,1)S(1)}, bf16[4,512]{1,0:T(4,128)(2,1)}, u32[]{:S(2)}) copy-start(bf16[4,512]{1,0:T(4,128)(2,1)} %param.21) | copy-start | bytes 12292
  14.5 7.0 %copy-start.9 = (bf16[4,1024]{1,0:T(4,128)(2,1)S(1)}, bf16[4,1024]{1,0:T(4,128)(2,1)}, u32[]{:S(2)}) copy-start(bf16[4,1024]{1,0:T(4,128)(2,1)} %param.23) | copy-start | bytes 24580
  14.5 7.0 %copy-start.8 = (bf16[2048,8]{0,1:T(8,128)(2,1)S(1)}, bf16[2048,8]{0,1:T(8,128)(2,1)}, u32[]{:S(2)}) copy-start(bf16[2048,8]{0,1:T(8,128)(2,1)} %param.20) | copy-start | bytes 98308
  14.5 7.4 %copy-start.13 = (bf16[128]{0:T(256)(128)(2,1)S(1)}, bf16[128]{0:T(256)(128)(2,1)}, u32[]{:S(2)}) copy-start(bf16[128]{0:T(256)(128)(2,1)} %param.24) | copy-start | bytes 772
  14.6 15.5 %collective-permute-start.3 = (bf16[3,512]{1,0:T(4,128)(2,1)S(1)}, bf16[3,512]{1,0:T(4,128)(2,1)S(1)}, u32[]{:S(2)}, u32[]{:S(2)}) collective-permute-start(bf16[3,512]{1,0:T(4,128)(2,1)S(1)} %slice.142), channel_id=1, source_target_pairs={{0,4},{4,8},{8,12},{12,16},{16,20},{20,24},{24,28},{28,32},{32,36}... | collective-permute-start | bytes 9224 | tf_op jit(solution)/shard_map/ppermute | solution.py:19
  19.5 16.7 %collective-permute-start.2 = (bf16[3,1024]{1,0:T(4,128)(2,1)S(1)}, bf16[3,1024]{1,0:T(4,128)(2,1)S(1)}, u32[]{:S(2)}, u32[]{:S(2)}) collective-permute-start(bf16[3,1024]{1,0:T(4,128)(2,1)S(1)} %slice.137), channel_id=1, source_target_pairs={{0,4},{4,8},{8,12},{12,16},{16,20},{20,24},{24,28},{28,32},{32,36}... | collective-permute-start | bytes 18440 | tf_op jit(solution)/shard_map/ppermute | solution.py:19
  33.2 2.9 copy-start.3
  33.2 3.0 copy-start.6
  136.2 2.8 copy-start.2
  187.9 2.8 copy-start.2
  239.6 2.8 copy-start.2
  250.5 9.8 %collective-permute-start = (bf16[8,128,128]{2,1,0:T(8,128)(2,1)S(1)}, bf16[8,128,128]{2,1,0:T(8,128)(2,1)S(1)}, u32[]{:S(2)}, u32[]{:S(2)}) collective-permute-start(bf16[8,128,128]{2,1,0:T(8,128)(2,1)S(1)} %fusion.131), channel_id=1, source_target_pairs={{0,4},{4,8},{8,12},{12,16},{16,20},{20,24},{24,28},{28,32},{32,36}... | collective-permute-start | bytes 786440 | tf_op jit(solution)/shard_map/while/body/eval_jaxpr/ppermute | solution.py:19
  263.1 9.8 %collective-permute-start = (bf16[8,128,128]{2,1,0:T(8,128)(2,1)S(1)}, bf16[8,128,128]{2,1,0:T(8,128)(2,1)S(1)}, u32[]{:S(2)}, u32[]{:S(2)}) collective-permute-start(bf16[8,128,128]{2,1,0:T(8,128)(2,1)S(1)} %fusion.131), channel_id=1, source_target_pairs={{0,4},{4,8},{8,12},{12,16},{16,20},{20,24},{24,28},{28,32},{32,36}... | collective-permute-start | bytes 786440 | tf_op jit(solution)/shard_map/while/body/eval_jaxpr/ppermute | solution.py:19
  275.8 9.8 %collective-permute-start = (bf16[8,128,128]{2,1,0:T(8,128)(2,1)S(1)}, bf16[8,128,128]{2,1,0:T(8,128)(2,1)S(1)}, u32[]{:S(2)}, u32[]{:S(2)}) collective-permute-start(bf16[8,128,128]{2,1,0:T(8,128)(2,1)S(1)} %fusion.131), channel_id=1, source_target_pairs={{0,4},{4,8},{8,12},{12,16},{16,20},{20,24},{24,28},{28,32},{32,36}... | collective-permute-start | bytes 786440 | tf_op jit(solution)/shard_map/while/body/eval_jaxpr/ppermute | solution.py:19
  288.4 9.8 %collective-permute-start = (bf16[8,128,128]{2,1,0:T(8,128)(2,1)S(1)}, bf16[8,128,128]{2,1,0:T(8,128)(2,1)S(1)}, u32[]{:S(2)}, u32[]{:S(2)}) collective-permute-start(bf16[8,128,128]{2,1,0:T(8,128)(2,1)S(1)} %fusion.131), channel_id=1, source_target_pairs={{0,4},{4,8},{8,12},{12,16},{16,20},{20,24},{24,28},{28,32},{32,36}... | collective-permute-start | bytes 786440 | tf_op jit(solution)/shard_map/while/body/eval_jaxpr/ppermute | solution.py:19
  301.1 9.8 %collective-permute-start = (bf16[8,128,128]{2,1,0:T(8,128)(2,1)S(1)}, bf16[8,128,128]{2,1,0:T(8,128)(2,1)S(1)}, u32[]{:S(2)}, u32[]{:S(2)}) collective-permute-start(bf16[8,128,128]{2,1,0:T(8,128)(2,1)S(1)} %fusion.131), channel_id=1, source_target_pairs={{0,4},{4,8},{8,12},{12,16},{16,20},{20,24},{24,28},{28,32},{32,36}... | collective-permute-start | bytes 786440 | tf_op jit(solution)/shard_map/while/body/eval_jaxpr/ppermute | solution.py:19
  313.7 9.8 %collective-permute-start = (bf16[8,128,128]{2,1,0:T(8,128)(2,1)S(1)}, bf16[8,128,128]{2,1,0:T(8,128)(2,1)S(1)}, u32[]{:S(2)}, u32[]{:S(2)}) collective-permute-start(bf16[8,128,128]{2,1,0:T(8,128)(2,1)S(1)} %fusion.131), channel_id=1, source_target_pairs={{0,4},{4,8},{8,12},{12,16},{16,20},{20,24},{24,28},{28,32},{32,36}... | collective-permute-start | bytes 786440 | tf_op jit(solution)/shard_map/while/body/eval_jaxpr/ppermute | solution.py:19
  326.4 9.8 %collective-permute-start = (bf16[8,128,128]{2,1,0:T(8,128)(2,1)S(1)}, bf16[8,128,128]{2,1,0:T(8,128)(2,1)S(1)}, u32[]{:S(2)}, u32[]{:S(2)}) collective-permute-start(bf16[8,128,128]{2,1,0:T(8,128)(2,1)S(1)} %fusion.131), channel_id=1, source_target_pairs={{0,4},{4,8},{8,12},{12,16},{16,20},{20,24},{24,28},{28,32},{32,36}... | collective-permute-start | bytes 786440 | tf_op jit(solution)/shard_map/while/body/eval_jaxpr/ppermute | solution.py:19
  339.0 9.8 %collective-permute-start = (bf16[8,128,128]{2,1,0:T(8,128)(2,1)S(1)}, bf16[8,128,128]{2,1,0:T(8,128)(2,1)S(1)}, u32[]{:S(2)}, u32[]{:S(2)}) collective-permute-start(bf16[8,128,128]{2,1,0:T(8,128)(2,1)S(1)} %fusion.131), channel_id=1, source_target_pairs={{0,4},{4,8},{8,12},{12,16},{16,20},{20,24},{24,28},{28,32},{32,36}... | collective-permute-start | bytes 786440 | tf_op jit(solution)/shard_map/while/body/eval_jaxpr/ppermute | solution.py:19
  351.7 9.8 %collective-permute-start = (bf16[8,128,128]{2,1,0:T(8,128)(2,1)S(1)}, bf16[8,128,128]{2,1,0:T(8,128)(2,1)S(1)}, u32[]{:S(2)}, u32[]{:S(2)}) collective-permute-start(bf16[8,128,128]{2,1,0:T(8,128)(2,1)S(1)} %fusion.131), channel_id=1, source_target_pairs={{0,4},{4,8},{8,12},{12,16},{16,20},{20,24},{24,28},{28,32},{32,36}... | collective-permute-start | bytes 786440 | tf_op jit(solution)/shard_map/while/body/eval_jaxpr/ppermute | solution.py:19
  364.3 9.8 %collective-permute-start = (bf16[8,128,128]{2,1,0:T(8,128)(2,1)S(1)}, bf16[8,128,128]{2,1,0:T(8,128)(2,1)S(1)}, u32[]{:S(2)}, u32[]{:S(2)}) collective-permute-start(bf16[8,128,128]{2,1,0:T(8,128)(2,1)S(1)} %fusion.131), channel_id=1, source_target_pairs={{0,4},{4,8},{8,12},{12,16},{16,20},{20,24},{24,28},{28,32},{32,36}... | collective-permute-start | bytes 786440 | tf_op jit(solution)/shard_map/while/body/eval_jaxpr/ppermute | solution.py:19
  377.0 9.8 %collective-permute-start = (bf16[8,128,128]{2,1,0:T(8,128)(2,1)S(1)}, bf16[8,128,128]{2,1,0:T(8,128)(2,1)S(1)}, u32[]{:S(2)}, u32[]{:S(2)}) collective-permute-start(bf16[8,128,128]{2,1,0:T(8,128)(2,1)S(1)} %fusion.131), channel_id=1, source_target_pairs={{0,4},{4,8},{8,12},{12,16},{16,20},{20,24},{24,28},{28,32},{32,36}... | collective-permute-start | bytes 786440 | tf_op jit(solution)/shard_map/while/body/eval_jaxpr/ppermute | solution.py:19
  389.6 9.8 %collective-permute-start = (bf16[8,128,128]{2,1,0:T(8,128)(2,1)S(1)}, bf16[8,128,128]{2,1,0:T(8,128)(2,1)S(1)}, u32[]{:S(2)}, u32[]{:S(2)}) collective-permute-start(bf16[8,128,128]{2,1,0:T(8,128)(2,1)S(1)} %fusion.131), channel_id=1, source_target_pairs={{0,4},{4,8},{8,12},{12,16},{16,20},{20,24},{24,28},{28,32},{32,36}... | collective-permute-start | bytes 786440 | tf_op jit(solution)/shard_map/while/body/eval_jaxpr/ppermute | solution.py:19
  402.3 9.8 %collective-permute-start = (bf16[8,128,128]{2,1,0:T(8,128)(2,1)S(1)}, bf16[8,128,128]{2,1,0:T(8,128)(2,1)S(1)}, u32[]{:S(2)}, u32[]{:S(2)}) collective-permute-start(bf16[8,128,128]{2,1,0:T(8,128)(2,1)S(1)} %fusion.131), channel_id=1, source_target_pairs={{0,4},{4,8},{8,12},{12,16},{16,20},{20,24},{24,28},{28,32},{32,36}... | collective-permute-start | bytes 786440 | tf_op jit(solution)/shard_map/while/body/eval_jaxpr/ppermute | solution.py:19
  414.9 9.8 %collective-permute-start = (bf16[8,128,128]{2,1,0:T(8,128)(2,1)S(1)}, bf16[8,128,128]{2,1,0:T(8,128)(2,1)S(1)}, u32[]{:S(2)}, u32[]{:S(2)}) collective-permute-start(bf16[8,128,128]{2,1,0:T(8,128)(2,1)S(1)} %fusion.131), channel_id=1, source_target_pairs={{0,4},{4,8},{8,12},{12,16},{16,20},{20,24},{24,28},{28,32},{32,36}... | collective-permute-start | bytes 786440 | tf_op jit(solution)/shard_map/while/body/eval_jaxpr/ppermute | solution.py:19
  427.6 9.8 %collective-permute-start = (bf16[8,128,128]{2,1,0:T(8,128)(2,1)S(1)}, bf16[8,128,128]{2,1,0:T(8,128)(2,1)S(1)}, u32[]{:S(2)}, u32[]{:S(2)}) collective-permute-start(bf16[8,128,128]{2,1,0:T(8,128)(2,1)S(1)} %fusion.131), channel_id=1, source_target_pairs={{0,4},{4,8},{8,12},{12,16},{16,20},{20,24},{24,28},{28,32},{32,36}... | collective-permute-start | bytes 786440 | tf_op jit(solution)/shard_map/while/body/eval_jaxpr/ppermute | solution.py:19
  440.2 9.8 %collective-permute-start = (bf16[8,128,128]{2,1,0:T(8,128)(2,1)S(1)}, bf16[8,128,128]{2,1,0:T(8,128)(2,1)S(1)}, u32[]{:S(2)}, u32[]{:S(2)}) collective-permute-start(bf16[8,128,128]{2,1,0:T(8,128)(2,1)S(1)} %fusion.131), channel_id=1, source_target_pairs={{0,4},{4,8},{8,12},{12,16},{16,20},{20,24},{24,28},{28,32},{32,36}... | collective-permute-start | bytes 786440 | tf_op jit(solution)/shard_map/while/body/eval_jaxpr/ppermute | solution.py:19
  452.9 9.8 %collective-permute-start = (bf16[8,128,128]{2,1,0:T(8,128)(2,1)S(1)}, bf16[8,128,128]{2,1,0:T(8,128)(2,1)S(1)}, u32[]{:S(2)}, u32[]{:S(2)}) collective-permute-start(bf16[8,128,128]{2,1,0:T(8,128)(2,1)S(1)} %fusion.131), channel_id=1, source_target_pairs={{0,4},{4,8},{8,12},{12,16},{16,20},{20,24},{24,28},{28,32},{32,36}... | collective-permute-start | bytes 786440 | tf_op jit(solution)/shard_map/while/body/eval_jaxpr/ppermute | solution.py:19
  465.5 9.8 %collective-permute-start = (bf16[8,128,128]{2,1,0:T(8,128)(2,1)S(1)}, bf16[8,128,128]{2,1,0:T(8,128)(2,1)S(1)}, u32[]{:S(2)}, u32[]{:S(2)}) collective-permute-start(bf16[8,128,128]{2,1,0:T(8,128)(2,1)S(1)} %fusion.131), channel_id=1, source_target_pairs={{0,4},{4,8},{8,12},{12,16},{16,20},{20,24},{24,28},{28,32},{32,36}... | collective-permute-start | bytes 786440 | tf_op jit(solution)/shard_map/while/body/eval_jaxpr/ppermute | solution.py:19
  478.2 9.8 %collective-permute-start = (bf16[8,128,128]{2,1,0:T(8,128)(2,1)S(1)}, bf16[8,128,128]{2,1,0:T(8,128)(2,1)S(1)}, u32[]{:S(2)}, u32[]{:S(2)}) collective-permute-start(bf16[8,128,128]{2,1,0:T(8,128)(2,1)S(1)} %fusion.131), channel_id=1, source_target_pairs={{0,4},{4,8},{8,12},{12,16},{16,20},{20,24},{24,28},{28,32},{32,36}... | collective-permute-start | bytes 786440 | tf_op jit(solution)/shard_map/while/body/eval_jaxpr/ppermute | solution.py:19
  490.8 9.8 %collective-permute-start = (bf16[8,128,128]{2,1,0:T(8,128)(2,1)S(1)}, bf16[8,128,128]{2,1,0:T(8,128)(2,1)S(1)}, u32[]{:S(2)}, u32[]{:S(2)}) collective-permute-start(bf16[8,128,128]{2,1,0:T(8,128)(2,1)S(1)} %fusion.131), channel_id=1, source_target_pairs={{0,4},{4,8},{8,12},{12,16},{16,20},{20,24},{24,28},{28,32},{32,36}... | collective-permute-start | bytes 786440 | tf_op jit(solution)/shard_map/while/body/eval_jaxpr/ppermute | solution.py:19
  503.5 9.8 %collective-permute-start = (bf16[8,128,128]{2,1,0:T(8,128)(2,1)S(1)}, bf16[8,128,128]{2,1,0:T(8,128)(2,1)S(1)}, u32[]{:S(2)}, u32[]{:S(2)}) collective-permute-start(bf16[8,128,128]{2,1,0:T(8,128)(2,1)S(1)} %fusion.131), channel_id=1, source_target_pairs={{0,4},{4,8},{8,12},{12,16},{16,20},{20,24},{24,28},{28,32},{32,36}... | collective-permute-start | bytes 786440 | tf_op jit(solution)/shard_map/while/body/eval_jaxpr/ppermute | solution.py:19
  516.1 9.8 %collective-permute-start = (bf16[8,128,128]{2,1,0:T(8,128)(2,1)S(1)}, bf16[8,128,128]{2,1,0:T(8,128)(2,1)S(1)}, u32[]{:S(2)}, u32[]{:S(2)}) collective-permute-start(bf16[8,128,128]{2,1,0:T(8,128)(2,1)S(1)} %fusion.131), channel_id=1, source_target_pairs={{0,4},{4,8},{8,12},{12,16},{16,20},{20,24},{24,28},{28,32},{32,36}... | collective-permute-start | bytes 786440 | tf_op jit(solution)/shard_map/while/body/eval_jaxpr/ppermute | solution.py:19
  528.8 9.8 %collective-permute-start = (bf16[8,128,128]{2,1,0:T(8,128)(2,1)S(1)}, bf16[8,128,128]{2,1,0:T(8,128)(2,1)S(1)}, u32[]{:S(2)}, u32[]{:S(2)}) collective-permute-start(bf16[8,128,128]{2,1,0:T(8,128)(2,1)S(1)} %fusion.131), channel_id=1, source_target_pairs={{0,4},{4,8},{8,12},{12,16},{16,20},{20,24},{24,28},{28,32},{32,36}... | collective-permute-start | bytes 786440 | tf_op jit(solution)/shard_map/while/body/eval_jaxpr/ppermute | solution.py:19
  541.4 9.8 %collective-permute-start = (bf16[8,128,128]{2,1,0:T(8,128)(2,1)S(1)}, bf16[8,128,128]{2,1,0:T(8,128)(2,1)S(1)}, u32[]{:S(2)}, u32[]{:S(2)}) collective-permute-start(bf16[8,128,128]{2,1,0:T(8,128)(2,1)S(1)} %fusion.131), channel_id=1, source_target_pairs={{0,4},{4,8},{8,12},{12,16},{16,20},{20,24},{24,28},{28,32},{32,36}... | collective-permute-start | bytes 786440 | tf_op jit(solution)/shard_map/while/body/eval_jaxpr/ppermute | solution.py:19
  554.1 9.8 %collective-permute-start = (bf16[8,128,128]{2,1,0:T(8,128)(2,1)S(1)}, bf16[8,128,128]{2,1,0:T(8,128)(2,1)S(1)}, u32[]{:S(2)}, u32[]{:S(2)}) collective-permute-start(bf16[8,128,128]{2,1,0:T(8,128)(2,1)S(1)} %fusion.131), channel_id=1, source_target_pairs={{0,4},{4,8},{8,12},{12,16},{16,20},{20,24},{24,28},{28,32},{32,36}... | collective-permute-start | bytes 786440 | tf_op jit(solution)/shard_map/while/body/eval_jaxpr/ppermute | solution.py:19
  566.7 9.8 %collective-permute-start = (bf16[8,128,128]{2,1,0:T(8,128)(2,1)S(1)}, bf16[8,128,128]{2,1,0:T(8,128)(2,1)S(1)}, u32[]{:S(2)}, u32[]{:S(2)}) collective-permute-start(bf16[8,128,128]{2,1,0:T(8,128)(2,1)S(1)} %fusion.131), channel_id=1, source_target_pairs={{0,4},{4,8},{8,12},{12,16},{16,20},{20,24},{24,28},{28,32},{32,36}... | collective-permute-start | bytes 786440 | tf_op jit(solution)/shard_map/while/body/eval_jaxpr/ppermute | solution.py:19
  579.4 9.8 %collective-permute-start = (bf16[8,128,128]{2,1,0:T(8,128)(2,1)S(1)}, bf16[8,128,128]{2,1,0:T(8,128)(2,1)S(1)}, u32[]{:S(2)}, u32[]{:S(2)}) collective-permute-start(bf16[8,128,128]{2,1,0:T(8,128)(2,1)S(1)} %fusion.131), channel_id=1, source_target_pairs={{0,4},{4,8},{8,12},{12,16},{16,20},{20,24},{24,28},{28,32},{32,36}... | collective-permute-start | bytes 786440 | tf_op jit(solution)/shard_map/while/body/eval_jaxpr/ppermute | solution.py:19
  592.0 9.8 %collective-permute-start = (bf16[8,128,128]{2,1,0:T(8,128)(2,1)S(1)}, bf16[8,128,128]{2,1,0:T(8,128)(2,1)S(1)}, u32[]{:S(2)}, u32[]{:S(2)}) collective-permute-start(bf16[8,128,128]{2,1,0:T(8,128)(2,1)S(1)} %fusion.131), channel_id=1, source_target_pairs={{0,4},{4,8},{8,12},{12,16},{16,20},{20,24},{24,28},{28,32},{32,36}... | collective-permute-start | bytes 786440 | tf_op jit(solution)/shard_map/while/body/eval_jaxpr/ppermute | solution.py:19
  604.7 9.8 %collective-permute-start = (bf16[8,128,128]{2,1,0:T(8,128)(2,1)S(1)}, bf16[8,128,128]{2,1,0:T(8,128)(2,1)S(1)}, u32[]{:S(2)}, u32[]{:S(2)}) collective-permute-start(bf16[8,128,128]{2,1,0:T(8,128)(2,1)S(1)} %fusion.131), channel_id=1, source_target_pairs={{0,4},{4,8},{8,12},{12,16},{16,20},{20,24},{24,28},{28,32},{32,36}... | collective-permute-start | bytes 786440 | tf_op jit(solution)/shard_map/while/body/eval_jaxpr/ppermute | solution.py:19
  617.3 9.8 %collective-permute-start = (bf16[8,128,128]{2,1,0:T(8,128)(2,1)S(1)}, bf16[8,128,128]{2,1,0:T(8,128)(2,1)S(1)}, u32[]{:S(2)}, u32[]{:S(2)}) collective-permute-start(bf16[8,128,128]{2,1,0:T(8,128)(2,1)S(1)} %fusion.131), channel_id=1, source_target_pairs={{0,4},{4,8},{8,12},{12,16},{16,20},{20,24},{24,28},{28,32},{32,36}... | collective-permute-start | bytes 786440 | tf_op jit(solution)/shard_map/while/body/eval_jaxpr/ppermute | solution.py:19
  630.0 9.8 %collective-permute-start = (bf16[8,128,128]{2,1,0:T(8,128)(2,1)S(1)}, bf16[8,128,128]{2,1,0:T(8,128)(2,1)S(1)}, u32[]{:S(2)}, u32[]{:S(2)}) collective-permute-start(bf16[8,128,128]{2,1,0:T(8,128)(2,1)S(1)} %fusion.131), channel_id=1, source_target_pairs={{0,4},{4,8},{8,12},{12,16},{16,20},{20,24},{24,28},{28,32},{32,36}... | collective-permute-start | bytes 786440 | tf_op jit(solution)/shard_map/while/body/eval_jaxpr/ppermute | solution.py:19
  (7 other events, 14.9 us)
Sparse Core Ops, SparseCore 0:
  653.5 22.7 reduce-scatter.1
where the time goes:
time: 687 us; the launch traced here: 683 us
  waiting for transfers between devices  265 us (39%)
  other arithmetic  197 us (29%)
  matrix products  120 us (17%)
  starting transfers between devices  68.6 us (10%)
  local copies, waits for them, and re-layouts  17.5 us (3%)
  between operations  13.8 us (2%)
    ppermute x34, waiting for transfers between devices, from_behind(): return lax.ppermute(block, axis, route)  242 us
    another operation x8, other arithmetic, delta_block(): lax.linalg.triangular_solve(system, beta_gate[:, :, None] * values, left_...  160 us
    dot_general x56, matrix products, contract(): return jnp.einsum(form, left, right, precision=exact_mode)  100 us
    ppermute x34, starting transfers between devices, from_behind(): return lax.ppermute(block, axis, route)  68.6 us
    convert_element_type x31, other arithmetic, advance(): from_behind(outgoing.astype(jnp.bfloat16), 'seq', 1).astype(outgoing.dtype)  25.9 us
    reduce_scatter x1, waiting for transfers between devices, shards(): lax.psum_scatter(rounded.astype(jnp.bfloat16), 'head', scatter_dimension=...  22.9 us
  transfers between devices with their start and end apart: 35, of which 32 were waited for; matrix products, arithmetic and copies ran while one was open for 3% of the time, Pallas kernels for 0%

commit v1 on v0

v1 whole, which is shorter than its diff:
```python
import functools

import jax
import jax.numpy as jnp
from jax import lax
from jax.experimental import pallas as pl
from jax.experimental.pallas import tpu as pltpu
from jax.sharding import PartitionSpec as P

DK = 128
DV = 128
KER = 4
HALO = 16
eps_norm = 1e-06
F32 = jnp.float32
BF16 = jnp.bfloat16
MESH = pl.DeviceIdType.MESH


def mm(a, b):
    return jnp.dot(a, b, preferred_element_type=F32)


def mm_nt(a, b):
    return lax.dot_general(a, b, (((1,), (1,)), ((), ())), preferred_element_type=F32)


def mm_tn(a, b):
    return lax.dot_general(a, b, (((0,), (0,)), ((), ())), preferred_element_type=F32)


def silu(x):
    return x / (1.0 + jnp.exp(-x))


def unit_rows(x):
    return x * lax.rsqrt(jnp.sum(x * x, axis=-1, keepdims=True) + eps_norm)


def block_solve(systems, row, col):
    eye = (row == col).astype(F32)
    same = (row // 16) == (col // 16)
    low = [a.astype(BF16) for a in systems]
    powers = [jnp.where(same, -a, 0.0) for a in systems]
    solved = [eye + n for n in powers]
    powers = [n.astype(BF16) for n in powers]
    for _ in range(3):
        powers = [mm(n, n).astype(BF16) for n in powers]
        solved = [x + mm(x.astype(BF16), n) for x, n in zip(solved, powers)]
    size = 16
    while size < row.shape[0]:
        off = ((row // (2 * size)) == (col // (2 * size))) & ((row // size) != (col // size))
        rounded = [x.astype(BF16) for x in solved]
        cross = [mm(jnp.where(off, a, 0.0).astype(BF16), x).astype(BF16) for a, x in zip(low, rounded)]
        solved = [s - mm(x, c) for s, x, c in zip(solved, rounded, cross)]
        size *= 2
    return [x.astype(BF16) for x in solved]


def local_delta(queries, keys, values, betas):
    rows = queries.shape[0]
    row = lax.broadcasted_iota(jnp.int32, (rows, rows), 0)
    col = lax.broadcasted_iota(jnp.int32, (rows, rows), 1)
    qb, kb = queries.astype(BF16), keys.astype(BF16)
    gram = jnp.where(row > col, mm_nt(kb, kb), 0.0)
    attend = jnp.where(row >= col, mm_nt(qb, kb), 0.0).astype(BF16)
    inverses = block_solve([b * gram for b in betas], row, col)
    results = []
    for inv, b, v in zip(inverses, betas, values):
        sides = jnp.concatenate([b * keys, b * v], axis=1).astype(BF16)
        both = mm(inv, sides).astype(BF16)
        carry = mm_tn(kb, both)
        seen = mm(attend, both)
        results.append((seen[:, DK:], queries - seen[:, :DK], carry))
    return results


def local_kernel(hid, halo, wq, wk, wv, wb, cq, ck, cv, part_ref, ask_ref, carry_ref, ext_ref):
    rows = hid.shape[0]
    step = pl.program_id(0)
    h = hid[...]
    edge = halo[...]

    def project(w, taps):
        weights = w[...]
        width = weights.shape[1]
        ext_ref[:8, :width] = mm(edge, weights).astype(BF16).astype(F32)[HALO - 8 :]
        ext_ref[8:, :width] = mm(h, weights).astype(BF16).astype(F32)
        t = taps[...].astype(F32)
        summed = jnp.zeros((rows, width), F32)
        for j in range(KER):
            summed = summed + t[j : j + 1] * ext_ref[pl.ds(8 - KER + 1 + j, rows), :width]
        return silu(summed)

    queries = unit_rows(project(wq, cq))
    keys = unit_rows(project(wk, ck))
    values = project(wv, cv)
    group = values.shape[1] // DV
    beta = 0.05 + 0.15 / (1.0 + jnp.exp(-mm(h, wb[...])))
    lane = lax.broadcasted_iota(jnp.int32, beta.shape, 1)
    betas = [
        jnp.sum(jnp.where(lane == step * group + j, beta, 0.0), axis=1, keepdims=True)
        for j in range(group)
    ]
    parts = [values[:, j * DV : (j + 1) * DV] for j in range(group)]
    for j, (part, ask, carry) in enumerate(local_delta(queries, keys, parts, betas)):
        part_ref[:, j * DV : (j + 1) * DV] = part
        ask_ref[:, j * DV : (j + 1) * DV] = ask.astype(BF16)
        carry_ref[j] = carry.astype(BF16)


def local_call(hidden, halo, w_query, w_key, w_value, w_beta, c_query, c_key, c_value):
    rows, depth = hidden.shape
    heads_key = w_query.shape[1] // DK
    heads = w_value.shape[1] // DV
    group = heads // heads_key
    wide = group * DV
    whole = lambda shape: pl.BlockSpec(shape, lambda g: (0, 0))
    cols = lambda r, c: pl.BlockSpec((r, c), lambda g: (0, g))
    return pl.pallas_call(
        local_kernel,
        grid=(heads_key,),
        in_specs=[
            whole((rows, depth)),
            whole((HALO, depth)),
            cols(depth, DK),
            cols(depth, DK),
            cols(depth, wide),
            whole((depth, heads)),
            cols(KER, DK),
            cols(KER, DK),
            cols(KER, wide),
        ],
        out_specs=[
            cols(rows, wide),
            cols(rows, wide),
            pl.BlockSpec((group, DK, DK + DV), lambda g: (g, 0, 0)),
        ],
        out_shape=[
            jax.ShapeDtypeStruct((rows, heads * DV), F32),
            jax.ShapeDtypeStruct((rows, heads * DV), BF16),
            jax.ShapeDtypeStruct((heads, DK, DK + DV), BF16),
        ],
        scratch_shapes=[pltpu.VMEM((rows + 8, wide), F32)],
        name="local_rule",
    )(hidden, halo, w_query, w_key, w_value, w_beta, c_query, c_key, c_value)


def join(first, second):
    return first + second - mm(second[:, :DK].astype(BF16), first.astype(BF16))


def carry_kernel(
    members, groups, carry_ref, state_ref, got, total, total_got, start, s1, r1, s2, r2, s3, r3
):
    me = lax.axis_index("seq")
    slot = lax.rem(me, members)
    team = me // members
    barrier = pltpu.get_barrier_semaphore()
    peers = [team * members + lax.rem(slot + d, members) for d in range(1, members)]
    mates = [lax.rem(team + d, groups) * members + slot for d in range(1, groups)]
    for peer in peers + mates:
        pl.semaphore_signal(barrier, inc=1, device_id={"seq": peer}, device_id_type=MESH)
    pl.semaphore_wait(barrier, len(peers) + len(mates))

    def remote(src, dst, send, recv, peer):
        return pltpu.make_async_remote_copy(
            src_ref=src,
            dst_ref=dst,
            send_sem=send,
            recv_sem=recv,
            device_id={"seq": peer},
            device_id_type=MESH,
        )

    sends = []
    for d in range(1, members):
        to = lax.rem(slot + d, members)
        copy = remote(carry_ref.at[to], got.at[slot], s1.at[d], r1.at[slot], peers[d - 1])
        copy.start()
        sends.append(copy)
    got[slot] = carry_ref[slot]
    prefix = []
    running = None
    for i in range(members):

        @pl.when(slot != i)
        def _():
            remote(got.at[i], got.at[i], s1.at[0], r1.at[i], peers[0]).wait_recv()

        mine = got[i].astype(F32)
        prefix.append(running)
        running = mine if running is None else join(running, mine)
    total[...] = running.astype(BF16)
    for d in range(1, groups):
        copy = remote(total, total_got.at[team], s2.at[d], r2.at[team], mates[d - 1])
        copy.start()
        sends.append(copy)
    total_got[team] = running.astype(BF16)
    state = jnp.zeros((DK, DV), F32)
    entry = state
    for i in range(groups):

        @pl.when(team != i)
        def _():
            remote(total_got.at[i], total_got.at[i], s2.at[0], r2.at[i], mates[0]).wait_recv()

        entry = jnp.where(team == i, state, entry)
        if i < groups - 1:
            whole = total_got[i].astype(F32)
            state = state + whole[:, DK:] - mm(whole[:, :DK].astype(BF16), state.astype(BF16))
    rounded = entry.astype(BF16)
    for i in range(members):
        begin = entry
        if i > 0:
            begin = entry + prefix[i][:, DK:] - mm(prefix[i][:, :DK].astype(BF16), rounded)
        start[i] = begin.astype(BF16)
    for d in range(1, members):
        to = lax.rem(slot + d, members)
        copy = remote(start.at[to], state_ref.at[slot], s3.at[d], r3.at[slot], peers[d - 1])
        copy.start()
        sends.append(copy)
    state_ref[slot] = start[slot]
    for i in range(members):

        @pl.when(slot != i)
        def _():
            remote(state_ref.at[i], state_ref.at[i], s3.at[0], r3.at[i], peers[0]).wait_recv()

    for copy in sends:
        copy.wait_send()


def carry_call(carry, size_seq):
    heads = carry.shape[0]
    members, groups = heads, size_seq // heads
    dma = pltpu.SemaphoreType.DMA
    return pl.pallas_call(
        functools.partial(carry_kernel, members, groups),
        in_specs=[pl.BlockSpec(memory_space=pltpu.VMEM)],
        out_specs=pl.BlockSpec(memory_space=pltpu.VMEM),
        out_shape=jax.ShapeDtypeStruct((heads, DK, DV), BF16),
        scratch_shapes=[
            pltpu.VMEM((members, DK, DK + DV), BF16),
            pltpu.VMEM((DK, DK + DV), BF16),
            pltpu.VMEM((groups, DK, DK + DV), BF16),
            pltpu.VMEM((members, DK, DV), BF16),
            dma((members,)),
            dma((members,)),
            dma((groups,)),
            dma((groups,)),
            dma((members,)),
            dma((members,)),
        ],
        compiler_params=pltpu.CompilerParams(collective_id=0, has_side_effects=True),
        name="carry_scan",
    )(carry)


def gated_kernel(part_ref, ask_ref, state_ref, gate_ref, gain_ref, w_ref, out_ref, gated_ref):
    @pl.when(pl.program_id(0) == 0)
    def _():
        gain = gain_ref[...].astype(F32)
        for i in range(state_ref.shape[0]):
            at = slice(i * DV, (i + 1) * DV)
            attended = part_ref[:, at] + mm(ask_ref[:, at], state_ref[i])
            scale = lax.rsqrt(jnp.mean(attended * attended, axis=-1, keepdims=True) + eps_norm)
            gate = silu(gate_ref[:, at].astype(F32))
            gated_ref[:, at] = (attended * scale * gain * gate).astype(BF16)

    out_ref[0] = mm(gated_ref[...], w_ref[...]).astype(BF16)


def gated_call(part, ask, state, gate, gain, w_out, size_head):
    rows, wide = part.shape
    heads = state.shape[0]
    tile = w_out.shape[1] // size_head
    return pl.pallas_call(
        gated_kernel,
        grid=(size_head,),
        in_specs=[
            pl.BlockSpec((rows, wide), lambda n: (0, 0)),
            pl.BlockSpec((rows, wide), lambda n: (0, 0)),
            pl.BlockSpec((heads, DK, DV), lambda n: (0, 0, 0)),
            pl.BlockSpec((rows, wide), lambda n: (0, 0)),
            pl.BlockSpec((1, DV), lambda n: (0, 0)),
            pl.BlockSpec((wide, tile), lambda n: (0, n)),
        ],
        out_specs=pl.BlockSpec((1, rows, tile), lambda n: (n, 0, 0)),
        out_shape=jax.ShapeDtypeStruct((size_head, rows, tile), BF16),
        scratch_shapes=[pltpu.VMEM((rows, wide), BF16)],
        name="gated_out",
    )(part, ask, state, gate, gain, w_out)


def shares_kernel(count, part_ref, out_ref, got, send, recv):
    me = lax.axis_index("head")
    barrier = pltpu.get_barrier_semaphore()
    peers = [lax.rem(me + d, count) for d in range(1, count)]
    for peer in peers:
        pl.semaphore_signal(barrier, inc=1, device_id={"head": peer}, device_id_type=MESH)
    pl.semaphore_wait(barrier, count - 1)
    copies = []
    for d in range(1, count):
        copy = pltpu.make_async_remote_copy(
            src_ref=part_ref.at[peers[d - 1]],
            dst_ref=got.at[d],
            send_sem=send.at[d],
            recv_sem=recv.at[d],
            device_id={"head": peers[d - 1]},
            device_id_type=MESH,
        )
        copy.start()
        copies.append(copy)
    total = part_ref[me].astype(F32)
    for d in range(1, count):
        copies[d - 1].wait_recv()
        total = total + got[d].astype(F32)
    out_ref[...] = total.astype(BF16)
    for copy in copies:
        copy.wait_send()


def shares_call(part):
    count, rows, tile = part.shape
    return pl.pallas_call(
        functools.partial(shares_kernel, count),
        in_specs=[pl.BlockSpec(memory_space=pltpu.VMEM)],
        out_specs=pl.BlockSpec(memory_space=pltpu.VMEM),
        out_shape=jax.ShapeDtypeStruct((rows, tile), BF16),
        scratch_shapes=[
            pltpu.VMEM((count, rows, tile), BF16),
            pltpu.SemaphoreType.DMA((count,)),
            pltpu.SemaphoreType.DMA((count,)),
        ],
        compiler_params=pltpu.CompilerParams(collective_id=1, has_side_effects=True),
        name="share_sum",
    )(part)


def shards(
    hidden,
    w_query,
    w_key,
    w_value,
    w_gate,
    w_beta,
    conv_query,
    conv_key,
    conv_value,
    norm_gain,
    w_out,
):
    rows = hidden.shape[0]
    size_seq = lax.axis_size("seq")
    halo = lax.ppermute(
        hidden[rows - HALO :], "seq", [(i, i + 1) for i in range(size_seq - 1)]
    )
    gate = jnp.dot(hidden, w_gate, preferred_element_type=F32).astype(BF16)
    part, ask, carry = local_call(
        hidden, halo, w_query, w_key, w_value, w_beta, conv_query, conv_key, conv_value
    )
    state = carry_call(carry, size_seq)
    partial = gated_call(
        part, ask, state, gate, norm_gain.reshape(1, DV), w_out, lax.axis_size("head")
    )
    return shares_call(partial)


def solution(mesh):
    in_specs = (
        P("seq", None),
        P(None, "head"),
        P(None, "head"),
        P(None, "head"),
        P(None, "head"),
        P(None, "head"),
        P(None, "head"),
        P(None, "head"),
        P(None, "head"),
        P(),
        P("head", None),
    )
    out_specs = P("seq", "head")
    return jax.shard_map(shards, mesh=mesh, in_specs=in_specs, out_specs=out_specs, check_vma=False)
```

time: 687 us -> 86.3 us (0.13)
  the two profiles are of different devices: /device:TPU:64 before, /device:TPU:1 now
where the time goes in v1:
time: 86.3 us; the launch traced here: 85.9 us
  Pallas kernels  72.7 us (84%)
  matrix products  4.56 us (5%)
  starting transfers between devices  4.5 us (5%)
  local copies, waits for them, and re-layouts  4.15 us (5%)
    pallas_call x1, Pallas kernels, carry_call(): pl.pallas_call(functools.partial(carry_kernel, members, groups), in_specs...  27.1 us
    pallas_call x1, Pallas kernels, local_call(): pl.pallas_call(local_kernel, grid=(heads_key,), in_specs=[whole((rows, de...  21.6 us
    pallas_call x1, Pallas kernels, shares_call(): pl.pallas_call(functools.partial(shares_kernel, count), in_specs=[pl.Bloc...  17.7 us
    pallas_call x1, Pallas kernels, gated_call(): pl.pallas_call(gated_kernel, grid=(size_head,), in_specs=[pl.BlockSpec((r...  6.25 us
    dot_general x1, matrix products, shards(): gate = jnp.dot(hidden, w_gate, preferred_element_type=F32).astype(BF16)  4.56 us
    ppermute x1, starting transfers between devices, shards(): lax.ppermute(hidden[rows - HALO:], 'seq', [(i, i + 1) for i in range(size...  4.5 us
    unnamed x6, local copies, waits for them, and re-layouts  3.3 us
  transfers between devices with their start and end apart: 1, of which 0 were waited for; matrix products, arithmetic and copies ran while one was open for 6% of the time, Pallas kernels for 0%

profile of v1, /device:TPU:1, one launch (start us, length us, event | category | flops | bytes accessed | tf_op | source)
XLA Modules:
  0.0 85.9 jit_solution(11113384003859731874)
XLA Ops:
  0.0 0.0 copy-start.1
  0.0 0.9 slice.3
  0.9 4.5 %collective-permute-start = (bf16[16,2048]{1,0:T(8,128)(2,1)S(1)}, bf16[16,2048]{1,0:T(8,128)(2,1)S(1)}, u32[]{:S(2)}, u32[]{:S(2)}) collective-permute-start(bf16[16,2048]{1,0:T(8,128)(2,1)S(1)} %slice.3), channel_id=1, source_target_pairs={{0,4},{4,8},{8,12},{12,16},{16,20},{20,24},{24,28},{28,32},{32,36}... | collective-permute-start | bytes 196616 | tf_op jit(solution)/shard_map/ppermute | solution.py:356
  5.4 4.6 %convolution_convert_fusion.gate_ref = bf16[256,1024]{1,0:T(8,128)(2,1)} fusion(bf16[256,2048]{1,0:T(8,128)(2,1)} %hid.1, bf16[2048,1024]{1,0:T(8,128)(2,1)} %param.15), kind=kOutput, calls=%fused_computation | convolution fusion | flops 1074003968 | bytes 5767168 | tf_op jit(solution)/shard_map/dot_general | solution.py:359
  9.9 0.0 copy-done.1
  9.9 1.0 %copy.12.wb = bf16[2048,8]{1,0:T(8,128)(2,1)} copy(bf16[2048,8]{0,1:T(8,128)(2,1)S(1)} %copy-done.1) | data formatting | bytes 65536 | tf_op args[5]
  10.9 0.0 collective-permute-done.halo
  10.9 0.0 copy-start
  10.9 0.6 copy-done
  11.6 21.6 %local_rule.1 = (f32[256,1024]{1,0:T(8,128)}, bf16[256,1024]{1,0:T(8,128)(2,1)}, bf16[8,128,256]{2,1,0:T(8,128)(2,1)}) custom-call(bf16[256,2048]{1,0:T(8,128)(2,1)} %hid.1, bf16[16,2048]{1,0:T(8,128)(2,1)} %copy-done, bf16[2048,512]{1,0:T(8,128)(2,1)} %wq.1, bf16[2048,512]{1,0:T(8,128)(2,1)} %wk.1, bf16[2048,1024]{1,0:T(8,128)(2,1)} %wv.1, ...), custom_call_target="tpu_custom_call" | custom-call | tf_op jit(solution)/shard_map/local_rule/pallas_call | solution.py:120
  33.2 27.1 %carry_scan.1.state_ref = bf16[8,128,128]{2,1,0:T(8,128)(2,1)} custom-call(bf16[8,128,256]{2,1,0:T(8,128)(2,1)} %get-tuple-element.10.carry_ref), custom_call_target="tpu_custom_call" | custom-call | tf_op jit(solution)/shard_map/carry_scan/pallas_call | solution.py:238
  60.3 6.2 %gated_out.1.part_ref = bf16[4,256,512]{2,1,0:T(8,128)(2,1)} custom-call(f32[256,1024]{1,0:T(8,128)} %get-tuple-element.8.part_ref, bf16[256,1024]{1,0:T(8,128)(2,1)} %get-tuple-element.9.ask_ref, bf16[8,128,128]{2,1,0:T(8,128)(2,1)} %carry_scan.1.state_ref, bf16[256,1024]{1,0:T(8,128)(2,1)} %convolution_convert_fusion.gate_ref, bf16[1,128]{1,0:T(2,128)(2,1)} %bitcast.3, ...), custom_call_target="tpu_custom_call" | custom-call | tf_op jit(solution)/shard_map/gated_out/pallas_call | solution.py:278
  66.5 17.7 %share_sum.1 = bf16[256,512]{1,0:T(8,128)(2,1)} custom-call(bf16[4,256,512]{2,1,0:T(8,128)(2,1)} %gated_out.1.part_ref), custom_call_target="tpu_custom_call" | custom-call | tf_op jit(solution)/shard_map/share_sum/pallas_call | solution.py:326
  84.2 1.7 %copy.14 = bf16[256,512]{1,0:T(8,128)(2,1)} copy(bf16[256,512]{1,0:T(8,128)(2,1)} %share_sum.1) | data formatting | bytes 524288
Async XLA Ops:
  0.0 9.9 %copy-start.1 = (bf16[2048,8]{0,1:T(8,128)(2,1)S(1)}, bf16[2048,8]{0,1:T(8,128)(2,1)}, u32[]{:S(2)}) copy-start(bf16[2048,8]{0,1:T(8,128)(2,1)} %param.16) | copy-start | bytes 98308
  0.9 10.1 %collective-permute-start = (bf16[16,2048]{1,0:T(8,128)(2,1)S(1)}, bf16[16,2048]{1,0:T(8,128)(2,1)S(1)}, u32[]{:S(2)}, u32[]{:S(2)}) collective-permute-start(bf16[16,2048]{1,0:T(8,128)(2,1)S(1)} %slice.3), channel_id=1, source_target_pairs={{0,4},{4,8},{8,12},{12,16},{16,20},{20,24},{24,28},{28,32},{32,36}... | collective-permute-start | bytes 196616 | tf_op jit(solution)/shard_map/ppermute | solution.py:356
  10.9 0.6 copy-start

commit v2 on v0

v2 whole, which is shorter than its diff:
```python
import functools

import jax
import jax.numpy as jnp
from jax import lax
from jax.experimental import pallas as pl
from jax.experimental.pallas import tpu as pltpu
from jax.sharding import PartitionSpec as P

DK = 128
DV = 128
KER = 4
HALO = 16
eps_norm = 1e-06
F32 = jnp.float32
BF16 = jnp.bfloat16
MESH = pl.DeviceIdType.MESH


def mm(a, b):
    return jnp.dot(a, b, preferred_element_type=F32)


def mm_nt(a, b):
    return lax.dot_general(a, b, (((1,), (1,)), ((), ())), preferred_element_type=F32)


def mm_tn(a, b):
    return lax.dot_general(a, b, (((0,), (0,)), ((), ())), preferred_element_type=F32)


def sigmoid(x):
    return 0.5 + 0.5 * jnp.tanh(0.5 * x)


def silu(x):
    half = 0.5 * x
    return half + half * jnp.tanh(half)


def unit_rows(x):
    return x * lax.rsqrt(jnp.sum(x * x, axis=-1, keepdims=True) + eps_norm)


def block_solve(systems, rounded, row, col):
    eye = (row == col).astype(F32)
    same = (row // 16) == (col // 16)
    powers = [jnp.where(same, -a, 0.0) for a in systems]
    solved = [eye + n for n in powers]
    powers = [n.astype(BF16) for n in powers]
    for _ in range(3):
        powers = [mm(n, n).astype(BF16) for n in powers]
        solved = [x + mm(x.astype(BF16), n) for x, n in zip(solved, powers)]
    size = 16
    while size < row.shape[0]:
        off = ((row // (2 * size)) == (col // (2 * size))) & ((row // size) != (col // size))
        halves = [x.astype(BF16) for x in solved]
        zero = jnp.zeros((), BF16)
        cross = [mm(jnp.where(off, a, zero), x).astype(BF16) for a, x in zip(rounded, halves)]
        solved = [s - mm(x, c) for s, x, c in zip(solved, halves, cross)]
        size *= 2
    return [x.astype(BF16) for x in solved]


def local_delta(queries, keys, values, betas):
    rows = queries[0].shape[0]
    half = rows // 2
    row = lax.broadcasted_iota(jnp.int32, (half, half), 0)
    col = lax.broadcasted_iota(jnp.int32, (half, half), 1)
    qb = [q.astype(BF16) for q in queries]
    kb = [k.astype(BF16) for k in keys]
    grams = [mm_nt(k, k) for k in kb]
    scores = [mm_nt(q, k) for q, k in zip(qb, kb)]
    systems, corners = [], []
    for gram, many in zip(grams, betas):
        first = jnp.where(row > col, gram[:half, :half], 0.0)
        last = jnp.where(row > col, gram[half:, half:], 0.0)
        for b in many:
            systems += [b[:half] * first, b[half:] * last]
            corners.append((b[half:] * gram[half:, :half]).astype(BF16))
    inverses = block_solve(systems, [a.astype(BF16) for a in systems], row, col)
    sides = []
    for k, vs, bs in zip(keys, values, betas):
        sides += [jnp.concatenate([b * k, b * v], axis=1) for b, v in zip(bs, vs)]
    tops = [mm(x, s[:half].astype(BF16)).astype(BF16) for x, s in zip(inverses[::2], sides)]
    rest = [(s[half:] - mm(c, t)).astype(BF16) for s, c, t in zip(sides, corners, tops)]
    ends = [mm(x, r).astype(BF16) for x, r in zip(inverses[1::2], rest)]
    results = []
    at = 0
    for q, k, score, many in zip(queries, kb, scores, betas):
        upper = jnp.where(row >= col, score[:half, :half], 0.0).astype(BF16)
        lower = jnp.concatenate(
            [score[half:, :half], jnp.where(row >= col, score[half:, half:], 0.0)], axis=1
        ).astype(BF16)
        for _ in many:
            both = jnp.concatenate([tops[at], ends[at]], axis=0)
            carry = mm_tn(k, both)
            seen = jnp.concatenate([mm(upper, tops[at]), mm(lower, both)], axis=0)
            results.append((seen[:, DK:], q - seen[:, :DK], carry))
            at += 1
    return results


def join(first, second):
    return first + second - mm(second[:, :DK].astype(BF16), first.astype(BF16))


def layer_kernel(
    sizes, hid, wq, wk, wv, wg, wb, cq, ck, cv, gain, wo, out_ref, bufs, rule, scan, shares
):
    size_seq, size_head, members = sizes
    groups = size_seq // members
    me, row_at = lax.axis_index("seq"), lax.axis_index("head")
    slot, team = lax.rem(me, members), me // members
    after, before = lax.rem(me + 1, size_seq), lax.rem(me + size_seq - 1, size_seq)
    peers = [team * members + lax.rem(slot + d, members) for d in range(1, members)]
    mates = [lax.rem(team + d, groups) * members + slot for d in range(1, groups)]
    others = [lax.rem(row_at + d, size_head) for d in range(1, size_head)]

    def remote(src, dst, send, recv, to):
        return pltpu.make_async_remote_copy(
            src_ref=src, dst_ref=dst, send_sem=send, recv_sem=recv, device_id=to, device_id_type=MESH
        )

    h_buf, q_buf, k_buf, v_buf, g_buf, o_buf, halo, load_sem, edge_send, edge_recv = bufs
    loads = []
    for i, (src, dst) in enumerate(
        ((hid, h_buf), (wq, q_buf), (wk, k_buf), (wv, v_buf), (wg, g_buf), (wo, o_buf))
    ):
        copy = pltpu.make_async_copy(src, dst, load_sem.at[i])
        copy.start()
        loads.append(copy)

    barrier = pltpu.get_barrier_semaphore()
    greeted = [{"seq": i} for i in [after, before] + peers + mates]
    greeted += [{"head": i} for i in (others[0], others[-1])]
    for to in greeted:
        pl.semaphore_signal(barrier, inc=1, device_id=to, device_id_type=MESH)
    pl.semaphore_wait(barrier, len(greeted))

    rows = h_buf.shape[0]
    edge = remote(hid.at[pl.ds(rows - HALO, HALO)], halo, edge_send, edge_recv, {"seq": after})
    edge.start()

    ext_ref, part_ref, ask_ref, carry_ref = rule
    loads[0].wait()
    h = h_buf[...]
    beta = 0.05 + 0.15 * sigmoid(mm_nt(h, wb[...]))
    lane = lax.broadcasted_iota(jnp.int32, beta.shape, 1)
    betas = [
        jnp.sum(jnp.where(lane == j, beta, 0.0), axis=1, keepdims=True)
        for j in range(beta.shape[1])
    ]
    edge.wait_recv()
    border = halo[...]
    tall = jnp.concatenate([jnp.where(me > 0, border, jnp.zeros_like(border)), h], axis=0)

    def project(load, w, taps):
        load.wait()
        width = w.shape[1]
        ext_ref[:, :width] = mm(tall, w[...]).astype(BF16).astype(F32)[HALO - 8 :]
        t = taps[...].astype(F32)
        summed = jnp.zeros((rows, width), F32)
        for j in range(KER):
            summed = summed + t[j : j + 1] * ext_ref[pl.ds(8 - KER + 1 + j, rows), :width]
        return silu(summed)

    split = lambda x: [x[:, j * DK : (j + 1) * DK] for j in range(x.shape[1] // DK)]
    queries = [unit_rows(x) for x in split(project(loads[1], q_buf, cq))]
    keys = [unit_rows(x) for x in split(project(loads[2], k_buf, ck))]
    values = split(project(loads[3], v_buf, cv))
    heads = len(values)
    group = heads // len(keys)
    nest = lambda x: [x[j : j + group] for j in range(0, len(x), group)]
    for j, (part, ask, carry) in enumerate(
        local_delta(queries, keys, nest(values), nest(betas))
    ):
        part_ref[:, j * DV : (j + 1) * DV] = part
        ask_ref[:, j * DV : (j + 1) * DV] = ask.astype(BF16)
        carry_ref[j] = carry.astype(BF16)

    got, total, total_got, start, state_ref, s1, r1, s2, r2, s3, r3 = scan
    sends = []
    for d in range(1, members):
        to = lax.rem(slot + d, members)
        copy = remote(carry_ref.at[to], got.at[slot], s1.at[d], r1.at[slot], {"seq": peers[d - 1]})
        copy.start()
        sends.append(copy)
    got[slot] = carry_ref[slot]

    gate_ref, gated_ref, keep, relay, opp, direct, hop, land, sr, rr = shares
    loads[4].wait()
    gain_row = gain[...].astype(F32)
    gate = silu(mm(h, g_buf[...]).astype(BF16).astype(F32))
    for j in range(heads):
        at = slice(j * DV, (j + 1) * DV)
        gate_ref[:, at] = gate[:, at] * gain_row

    prefix = []
    running = None
    for i in range(members):

        @pl.when(slot != i)
        def _():
            remote(got.at[i], got.at[i], s1.at[0], r1.at[i], {"seq": peers[0]}).wait_recv()

        mine = got[i].astype(F32)
        prefix.append(running)
        running = mine if running is None else join(running, mine)
    total[...] = running.astype(BF16)
    for d in range(1, groups):

        @pl.when(team + d < groups)
        def _():
            remote(
                total, total_got.at[team], s2.at[d], r2.at[team], {"seq": mates[d - 1]}
            ).start()

    state = jnp.zeros((DK, DV), F32)
    entry = state
    for i in range(groups - 1):

        @pl.when(team > i)
        def _():
            remote(total_got.at[i], total_got.at[i], s2.at[0], r2.at[i], {"seq": mates[0]}).wait_recv()

        whole = total_got[i].astype(F32)
        moved = state + whole[:, DK:] - mm(whole[:, :DK].astype(BF16), state.astype(BF16))
        state = jnp.where(team > i, moved, state)
    entry = state
    rounded = entry.astype(BF16)
    for i in range(members):
        begin = entry
        if i > 0:
            begin = entry + prefix[i][:, DK:] - mm(prefix[i][:, :DK].astype(BF16), rounded)
        start[i] = begin.astype(BF16)
    for d in range(1, members):
        to = lax.rem(slot + d, members)
        copy = remote(
            start.at[to], state_ref.at[slot], s3.at[d], r3.at[slot], {"seq": peers[d - 1]}
        )
        copy.start()
        sends.append(copy)
    state_ref[slot] = start[slot]
    for i in range(members):

        @pl.when(slot != i)
        def _():
            remote(state_ref.at[i], state_ref.at[i], s3.at[0], r3.at[i], {"seq": peers[0]}).wait_recv()

        at = slice(i * DV, (i + 1) * DV)
        attended = part_ref[:, at] + mm(ask_ref[:, at], state_ref[i])
        scale = lax.rsqrt(jnp.mean(attended * attended, axis=-1, keepdims=True) + eps_norm)
        gated_ref[:, at] = (attended * scale * gate_ref[:, at]).astype(BF16)

    loads[5].wait()
    gated = gated_ref[...]
    tile = out_ref.shape[1]
    half = rows // 2
    upper, lower = pl.ds(0, half), pl.ds(half, half)

    def share(to):
        columns = pl.ds(pl.multiple_of(to * tile, tile), tile)
        return mm(gated, o_buf[:, columns]).astype(BF16)

    right, far, left = others
    opp[...] = share(far)
    hops = [
        remote(opp.at[upper], hop.at[upper], sr.at[0], rr.at[0], {"head": right}),
        remote(opp.at[lower], hop.at[lower], sr.at[1], rr.at[1], {"head": left}),
    ]
    for copy in hops:
        copy.start()
    to_right, to_left = share(right), share(left)
    keep[upper], keep[lower] = to_right[:half], to_left[half:]
    direct[lower], direct[upper] = to_right[half:], to_left[:half]
    lands = [
        remote(direct.at[lower], land.at[lower], sr.at[2], rr.at[2], {"head": right}),
        remote(direct.at[upper], land.at[upper], sr.at[3], rr.at[3], {"head": left}),
    ]
    for copy in lands:
        copy.start()
    ends = []
    for n, (at, to) in enumerate(((upper, right), (lower, left))):
        hops[n].wait_recv()
        relay[at] = (hop[at].astype(F32) + keep[at].astype(F32)).astype(BF16)
        copy = remote(relay.at[at], hop.at[pl.ds(rows + n * half, half)], sr.at[4 + n], rr.at[4 + n], {"head": to})
        copy.start()
        ends.append(copy)
    mine = share(row_at).astype(F32)
    for n, at in ((1, upper), (0, lower)):
        lands[n].wait_recv()
        ends[1 - n].wait_recv()
        top = 0 if n == 1 else half
        out_ref[at] = (
            mine[top : top + half] + land[at].astype(F32) + hop[pl.ds(rows + top, half)].astype(F32)
        ).astype(BF16)

    edge.wait_send()
    for copy in sends + hops + lands + ends:
        copy.wait_send()
    for d in range(1, groups):

        @pl.when(team + d < groups)
        def _():
            remote(
                total, total_got.at[team], s2.at[d], r2.at[team], {"seq": mates[d - 1]}
            ).wait_send()


def shards(
    hidden,
    w_query,
    w_key,
    w_value,
    w_gate,
    w_beta,
    conv_query,
    conv_key,
    conv_value,
    norm_gain,
    w_out,
):
    size_seq, size_head = lax.axis_size("seq"), lax.axis_size("head")
    rows, depth = hidden.shape
    wide = w_value.shape[1]
    heads = wide // DV
    groups = size_seq // heads
    tile = w_out.shape[1] // size_head
    vmem = pl.BlockSpec(memory_space=pltpu.VMEM)
    hbm = pl.BlockSpec(memory_space=pl.ANY)
    like = lambda a: pltpu.VMEM(a.shape, a.dtype)
    dma = pltpu.SemaphoreType.DMA
    bufs = [like(a) for a in (hidden, w_query, w_key, w_value, w_gate, w_out)]
    bufs += [pltpu.VMEM((HALO, depth), BF16), dma((6,)), dma, dma]
    rule = [
        pltpu.VMEM((rows + 8, wide), F32),
        pltpu.VMEM((rows, wide), F32),
        pltpu.VMEM((rows, wide), BF16),
        pltpu.VMEM((heads, DK, DK + DV), BF16),
    ]
    scan = [
        pltpu.VMEM((heads, DK, DK + DV), BF16),
        pltpu.VMEM((DK, DK + DV), BF16),
        pltpu.VMEM((groups, DK, DK + DV), BF16),
        pltpu.VMEM((heads, DK, DV), BF16),
        pltpu.VMEM((heads, DK, DV), BF16),
    ]
    scan += [dma((heads,)), dma((heads,)), dma((groups,)), dma((groups,)), dma((heads,)), dma((heads,))]
    shares = [pltpu.VMEM((rows, wide), F32), pltpu.VMEM((rows, wide), BF16)]
    shares += [pltpu.VMEM((rows, tile), BF16)] * 4
    shares += [pltpu.VMEM((2 * rows, tile), BF16), pltpu.VMEM((rows, tile), BF16), dma((6,)), dma((6,))]
    return pl.pallas_call(
        functools.partial(layer_kernel, (size_seq, size_head, heads)),
        in_specs=[hbm] * 5 + [vmem] * 5 + [hbm],
        out_specs=vmem,
        out_shape=jax.ShapeDtypeStruct((rows, tile), BF16),
        scratch_shapes=[bufs, rule, scan, shares],
        compiler_params=pltpu.CompilerParams(collective_id=0, has_side_effects=True),
        name="layer",
    )(
        hidden,
        w_query,
        w_key,
        w_value,
        w_gate,
        w_beta.T,
        conv_query,
        conv_key,
        conv_value,
        norm_gain.reshape(1, DV),
        w_out,
    )


def solution(mesh):
    in_specs = (
        P("seq", None),
        P(None, "head"),
        P(None, "head"),
        P(None, "head"),
        P(None, "head"),
        P(None, "head"),
        P(None, "head"),
        P(None, "head"),
        P(None, "head"),
        P(),
        P("head", None),
    )
    out_specs = P("seq", "head")
    return jax.shard_map(shards, mesh=mesh, in_specs=in_specs, out_specs=out_specs, check_vma=False)
```

time: 687 us -> 50.6 us (0.07)
  waiting for transfers between devices: 265 us -> 0 us
  other arithmetic: 197 us -> 0 us
  matrix products: 120 us -> 0 us
  starting transfers between devices: 68.6 us -> 0 us
  Pallas kernels: 0 us -> 48.7 us
  local copies, waits for them, and re-layouts: 17.5 us -> 1.67 us
  between operations: 13.8 us -> 0.01 us
    ppermute x34 -> x0, waiting for transfers between devices: 242 us -> none  [from_behind(): return lax.ppermute(block, axis, route)]
    another operation x8 -> x0, other arithmetic: 160 us -> none  [delta_block(): lax.linalg.triangular_solve(system, beta_gate[:, :, None] * values, left_...]
    dot_general x61 -> x0, matrix products: 114 us -> none  [the longest x56 100 us: contract(): return jnp.einsum(form, left, right, precision=exact_mode)]
    ppermute x34 -> x0, starting transfers between devices: 68.6 us -> none  [from_behind(): return lax.ppermute(block, axis, route)]
    pallas_call x0 -> x1, Pallas kernels: none -> 48.7 us  [shards(): pl.pallas_call(functools.partial(layer_kernel, (size_seq, size_head, head...]
    convert_element_type x36 -> x0, other arithmetic: 27.2 us -> none  [the longest x31 25.9 us: advance(): from_behind(outgoing.astype(jnp.bfloat16), 'seq', 1).astype(outgoing.dtype)]
    reduce_scatter x1 -> x0, waiting for transfers between devices: 22.9 us -> none  [shards(): lax.psum_scatter(rounded.astype(jnp.bfloat16), 'head', scatter_dimension=...]
  transfers between devices with their start and end apart: 35 -> 0, of which waited for: 32 -> 0; matrix products, arithmetic and copies ran while one was open for 3% -> 0% of each run, Pallas kernels for 0% -> 0%
where the time goes in v2:
time: 50.6 us; the launch traced here: 50.4 us
  Pallas kernels  48.7 us (96%)
  local copies, waits for them, and re-layouts  1.67 us (3%)
    pallas_call x1, Pallas kernels, shards(): pl.pallas_call(functools.partial(layer_kernel, (size_seq, size_head, head...  48.7 us
    unnamed x1, local copies, waits for them, and re-layouts  1.67 us

profile of v2, /device:TPU:64, one launch (start us, length us, event | category | flops | bytes accessed | tf_op | source)
XLA Modules:
  0.0 50.4 jit_solution(17094080935524456664)
XLA Ops:
  0.0 48.7 %layer.1 = bf16[256,512]{1,0:T(8,128)(2,1)} custom-call(bf16[256,2048]{1,0:T(8,128)(2,1)} %hid.1, bf16[2048,512]{1,0:T(8,128)(2,1)} %wq.1, bf16[2048,512]{1,0:T(8,128)(2,1)} %wk.1, bf16[2048,1024]{1,0:T(8,128)(2,1)} %wv.1, bf16[2048,1024]{1,0:T(8,128)(2,1)} %wg.1, bf16[8,2048]{1,0:T(8,128)(2,1)} %bitcast.2, bf16[4,512]{1,0:T(4,128)(2,1)} %cq.1, ...), custom_call_target="tpu_custom_call" | custom-call | tf_op jit(solution)/shard_map/layer/pallas_call | solution.py:353
  48.7 1.7 %copy.13 = bf16[256,512]{1,0:T(8,128)(2,1)} copy(bf16[256,512]{1,0:T(8,128)(2,1)} %layer.1) | data formatting | bytes 524288

commit v3 on v2

--- a/solution.py
+++ b/solution.py
@@ -11,6 +11,7 @@
 DV = 128
 KER = 4
 HALO = 16
+VALUE_PARTS = 2
 eps_norm = 1e-06
 F32 = jnp.float32
 BF16 = jnp.bfloat16
@@ -42,28 +43,59 @@
     return x * lax.rsqrt(jnp.sum(x * x, axis=-1, keepdims=True) + eps_norm)
 
 
-def block_solve(systems, rounded, row, col):
-    eye = (row == col).astype(F32)
-    same = (row // 16) == (col // 16)
-    powers = [jnp.where(same, -a, 0.0) for a in systems]
-    solved = [eye + n for n in powers]
-    powers = [n.astype(BF16) for n in powers]
-    for _ in range(3):
-        powers = [mm(n, n).astype(BF16) for n in powers]
-        solved = [x + mm(x.astype(BF16), n) for x, n in zip(solved, powers)]
+def block_solve(systems):
+    n = systems[0].shape[0]
+    row = lax.broadcasted_iota(jnp.int32, (n, n), 0)
+    col = lax.broadcasted_iota(jnp.int32, (n, n), 1)
+    zero = jnp.zeros((), BF16)
+
+    def pick(a, size, first, stride):
+        lane = lax.broadcasted_iota(jnp.int32, (size, n), 1) // size
+        out = jnp.zeros((size, n), F32)
+        for b in range(first, n // size, stride):
+            out = jnp.where(lane == b - first, a[b * size : (b + 1) * size], out)
+        return out
+
+    def spread(x, size, mask):
+        return jnp.where(mask, jnp.concatenate([x.astype(BF16)] * (n // size), axis=0), zero)
+
     size = 16
-    while size < row.shape[0]:
-        off = ((row // (2 * size)) == (col // (2 * size))) & ((row // size) != (col // size))
-        halves = [x.astype(BF16) for x in solved]
-        zero = jnp.zeros((), BF16)
-        cross = [mm(jnp.where(off, a, zero), x).astype(BF16) for a, x in zip(rounded, halves)]
-        solved = [s - mm(x, c) for s, x, c in zip(solved, halves, cross)]
+    same = (row // size) == (col // size)
+    small = lax.broadcasted_iota(jnp.int32, (size, n), 1) % size
+    eye = (small == lax.broadcasted_iota(jnp.int32, (size, n), 0)).astype(F32)
+    powers = [-pick(a, size, 0, 1) for a in systems]
+    solved = [eye + p for p in powers]
+    powers = [mm(p.astype(BF16), spread(p, size, same)) for p in powers]
+    for last in (False, False, True):
+        wide = [spread(p, size, same) for p in powers]
+        if last:
+            solved = [x + mm(x.astype(BF16), w) for x, w in zip(solved, wide)]
+        else:
+            both = [
+                mm(jnp.concatenate([x, p], axis=0).astype(BF16), w)
+                for x, p, w in zip(solved, powers, wide)
+            ]
+            solved = [x + y[:size] for x, y in zip(solved, both)]
+            powers = [y[size:] for y in both]
+    while size < n:
+        same = (row // size) == (col // size)
+        below = ((row // size) == (col // size) + 1) & ((row // size) % 2 == 1)
+        odd = (lax.broadcasted_iota(jnp.int32, (size, n), 1) // size) % 2 == 1
+        cross = [
+            mm(pick(a, size, 1, 2).astype(BF16), spread(x, size, same))
+            for a, x in zip(systems, solved)
+        ]
+        cross = [mm(x.astype(BF16), spread(c, size, below)) for x, c in zip(solved, cross)]
+        solved = [
+            jnp.concatenate([jnp.where(odd, 0.0, x), jnp.where(odd, x, -c)], axis=0)
+            for x, c in zip(solved, cross)
+        ]
         size *= 2
     return [x.astype(BF16) for x in solved]
 
 
-def local_delta(queries, keys, values, betas):
-    rows = queries[0].shape[0]
+def key_side(queries, keys, betas):
+    rows = keys[0].shape[0]
     half = rows // 2
     row = lax.broadcasted_iota(jnp.int32, (half, half), 0)
     col = lax.broadcasted_iota(jnp.int32, (half, half), 1)
@@ -78,27 +110,24 @@
         for b in many:
             systems += [b[:half] * first, b[half:] * last]
             corners.append((b[half:] * gram[half:, :half]).astype(BF16))
-    inverses = block_solve(systems, [a.astype(BF16) for a in systems], row, col)
-    sides = []
-    for k, vs, bs in zip(keys, values, betas):
-        sides += [jnp.concatenate([b * k, b * v], axis=1) for b, v in zip(bs, vs)]
-    tops = [mm(x, s[:half].astype(BF16)).astype(BF16) for x, s in zip(inverses[::2], sides)]
-    rest = [(s[half:] - mm(c, t)).astype(BF16) for s, c, t in zip(sides, corners, tops)]
-    ends = [mm(x, r).astype(BF16) for x, r in zip(inverses[1::2], rest)]
-    results = []
-    at = 0
-    for q, k, score, many in zip(queries, kb, scores, betas):
+    inverses = block_solve(systems)
+    masked = []
+    for score in scores:
         upper = jnp.where(row >= col, score[:half, :half], 0.0).astype(BF16)
         lower = jnp.concatenate(
             [score[half:, :half], jnp.where(row >= col, score[half:, half:], 0.0)], axis=1
         ).astype(BF16)
-        for _ in many:
-            both = jnp.concatenate([tops[at], ends[at]], axis=0)
-            carry = mm_tn(k, both)
-            seen = jnp.concatenate([mm(upper, tops[at]), mm(lower, both)], axis=0)
-            results.append((seen[:, DK:], q - seen[:, :DK], carry))
-            at += 1
-    return results
+        masked.append((upper, lower))
+    return kb, masked, list(zip(inverses[::2], inverses[1::2], corners))
+
+
+def value_side(solves, keys, values, betas):
+    half = keys[0].shape[0] // 2
+    sides = [jnp.concatenate([b * k, b * v], axis=1) for k, v, b in zip(keys, values, betas)]
+    tops = [mm(x[0], s[:half].astype(BF16)).astype(BF16) for x, s in zip(solves, sides)]
+    rest = [(s[half:] - mm(x[2], t)).astype(BF16) for s, x, t in zip(sides, solves, tops)]
+    ends = [mm(x[1], r).astype(BF16) for x, r in zip(solves, rest)]
+    return [jnp.concatenate(pair, axis=0) for pair in zip(tops, ends)]
 
 
 def join(first, second):
@@ -123,13 +152,17 @@
         )
 
     h_buf, q_buf, k_buf, v_buf, g_buf, o_buf, halo, load_sem, edge_send, edge_recv = bufs
-    loads = []
-    for i, (src, dst) in enumerate(
-        ((hid, h_buf), (wq, q_buf), (wk, k_buf), (wv, v_buf), (wg, g_buf), (wo, o_buf))
-    ):
-        copy = pltpu.make_async_copy(src, dst, load_sem.at[i])
+    rows, wide = h_buf.shape[0], v_buf.shape[1]
+    part_wide = wide // VALUE_PARTS
+    ways = [(hid, h_buf), (wk, k_buf), (wq, q_buf)]
+    for n in range(VALUE_PARTS):
+        at = pl.ds(n * part_wide, part_wide)
+        ways.append((wv.at[:, at], v_buf.at[:, at]))
+    ways += [(wg, g_buf), (wo, o_buf)]
+    loads = [pltpu.make_async_copy(src, dst, load_sem.at[i]) for i, (src, dst) in enumerate(ways)]
+    load_h, load_k, load_q, *load_v, load_g, load_o = loads
+    for copy in loads[:-2]:
         copy.start()
-        loads.append(copy)
 
     barrier = pltpu.get_barrier_semaphore()
     greeted = [{"seq": i} for i in [after, before] + peers + mates]
@@ -138,12 +171,11 @@
         pl.semaphore_signal(barrier, inc=1, device_id=to, device_id_type=MESH)
     pl.semaphore_wait(barrier, len(greeted))
 
-    rows = h_buf.shape[0]
     edge = remote(hid.at[pl.ds(rows - HALO, HALO)], halo, edge_send, edge_recv, {"seq": after})
     edge.start()
 
-    ext_ref, part_ref, ask_ref, carry_ref = rule
-    loads[0].wait()
+    ext_ref, ext_k, ext_q, part_ref, ask_ref, carry_ref = rule
+    load_h.wait()
     h = h_buf[...]
     beta = 0.05 + 0.15 * sigmoid(mm_nt(h, wb[...]))
     lane = lax.broadcasted_iota(jnp.int32, beta.shape, 1)
@@ -151,63 +183,100 @@
         jnp.sum(jnp.where(lane == j, beta, 0.0), axis=1, keepdims=True)
         for j in range(beta.shape[1])
     ]
+    def convolve(ext, taps, width):
+        t = 0.5 * taps.astype(F32)
+        summed = t[:1] * ext[pl.ds(8 - KER + 1, rows), :width]
+        for j in range(1, KER):
+            summed = summed + t[j : j + 1] * ext[pl.ds(8 - KER + 1 + j, rows), :width]
+        x = summed + summed * jnp.tanh(summed)
+        return [x[:, j * DK : (j + 1) * DK] for j in range(width // DK)]
+
+    load_k.wait()
+    ext_k[8:] = mm(h, k_buf[...])
+    load_q.wait()
+    ext_q[8:] = mm(h, q_buf[...])
     edge.wait_recv()
     border = halo[...]
-    tall = jnp.concatenate([jnp.where(me > 0, border, jnp.zeros_like(border)), h], axis=0)
-
-    def project(load, w, taps):
-        load.wait()
-        width = w.shape[1]
-        ext_ref[:, :width] = mm(tall, w[...]).astype(BF16).astype(F32)[HALO - 8 :]
-        t = taps[...].astype(F32)
-        summed = jnp.zeros((rows, width), F32)
-        for j in range(KER):
-            summed = summed + t[j : j + 1] * ext_ref[pl.ds(8 - KER + 1 + j, rows), :width]
-        return silu(summed)
-
-    split = lambda x: [x[:, j * DK : (j + 1) * DK] for j in range(x.shape[1] // DK)]
-    queries = [unit_rows(x) for x in split(project(loads[1], q_buf, cq))]
-    keys = [unit_rows(x) for x in split(project(loads[2], k_buf, ck))]
-    values = split(project(loads[3], v_buf, cv))
-    heads = len(values)
+    border = jnp.where(me > 0, border, jnp.zeros_like(border))
+    tall = jnp.concatenate([border, h], axis=0)
+    ext_k[:8] = mm(border, k_buf[...])[HALO - 8 :]
+    ext_q[:8] = mm(border, q_buf[...])[HALO - 8 :]
+    keys = [unit_rows(x) for x in convolve(ext_k, ck[...], k_buf.shape[1])]
+    queries = [unit_rows(x) for x in convolve(ext_q, cq[...], q_buf.shape[1])]
+    heads = len(betas)
     group = heads // len(keys)
-    nest = lambda x: [x[j : j + group] for j in range(0, len(x), group)]
-    for j, (part, ask, carry) in enumerate(
-        local_delta(queries, keys, nest(values), nest(betas))
-    ):
-        part_ref[:, j * DV : (j + 1) * DV] = part
-        ask_ref[:, j * DV : (j + 1) * DV] = ask.astype(BF16)
-        carry_ref[j] = carry.astype(BF16)
+    kb, masked, solves = key_side(
+        queries, keys, [betas[j : j + group] for j in range(0, heads, group)]
+    )
 
     got, total, total_got, start, state_ref, s1, r1, s2, r2, s3, r3 = scan
-    sends = []
-    for d in range(1, members):
-        to = lax.rem(slot + d, members)
-        copy = remote(carry_ref.at[to], got.at[slot], s1.at[d], r1.at[slot], {"seq": peers[d - 1]})
-        copy.start()
-        sends.append(copy)
-    got[slot] = carry_ref[slot]
-
+
+    def carry_copy(j):
+        return remote(
+            carry_ref.at[j], got.at[slot], s1.at[j], r1.at[slot], {"seq": team * members + j}
+        )
+
+    sides = []
+    per = heads // VALUE_PARTS
+    for n in range(VALUE_PARTS):
+        load_v[n].wait()
+        if n == VALUE_PARTS - 1:
+            load_g.start()
+            load_o.start()
+        at = pl.ds(n * part_wide, part_wide)
+        ext_ref[...] = mm(tall, v_buf[:, at])[HALO - 8 :]
+        values = convolve(ext_ref, cv[:, at], part_wide)
+        mine = range(n * per, (n + 1) * per)
+        some = value_side(
+            [solves[j] for j in mine],
+            [keys[j // group] for j in mine],
+            values,
+            [betas[j] for j in mine],
+        )
+        for j, side in zip(mine, some):
+            carry_ref[j] = mm_tn(kb[j // group], side).astype(BF16)
+
+            @pl.when(slot != j)
+            def _():
+                carry_copy(j).start()
+
+            @pl.when(slot == j)
+            def _():
+                got[j] = carry_ref[j]
+
+        sides += some
+
+    half = rows // 2
+    for j, side in enumerate(sides):
+        at = slice(j * DV, (j + 1) * DV)
+        upper, lower = masked[j // group]
+        seen = jnp.concatenate([mm(upper, side[:half]), mm(lower, side)], axis=0)
+        part_ref[:, at] = seen[:, DK:]
+        ask_ref[:, at] = (queries[j // group] - seen[:, :DK]).astype(BF16)
     gate_ref, gated_ref, keep, relay, opp, direct, hop, land, sr, rr = shares
-    loads[4].wait()
+    load_g.wait()
     gain_row = gain[...].astype(F32)
     gate = silu(mm(h, g_buf[...]).astype(BF16).astype(F32))
     for j in range(heads):
         at = slice(j * DV, (j + 1) * DV)
         gate_ref[:, at] = gate[:, at] * gain_row
 
-    prefix = []
-    running = None
+    sends = []
+    spans = []
     for i in range(members):
 
         @pl.when(slot != i)
         def _():
             remote(got.at[i], got.at[i], s1.at[0], r1.at[i], {"seq": peers[0]}).wait_recv()
 
-        mine = got[i].astype(F32)
-        prefix.append(running)
-        running = mine if running is None else join(running, mine)
-    total[...] = running.astype(BF16)
+        spans.append(got[i].astype(F32))
+    level = {(i, i + 1): x for i, x in enumerate(spans)}
+    size = 1
+    while size < members:
+        for i in range(0, members, 2 * size):
+            level[i, i + 2 * size] = join(level[i, i + size], level[i + size, i + 2 * size])
+        size *= 2
+    total[...] = level[0, members].astype(BF16)
     for d in range(1, groups):
 
         @pl.when(team + d < groups)
@@ -216,8 +285,13 @@
                 total, total_got.at[team], s2.at[d], r2.at[team], {"seq": mates[d - 1]}
             ).start()
 
+    prefix = [None]
+    for i in range(1, members):
+        size = i & -i
+        if i > size:
+            level[0, i] = join(level[0, i - size], level[i - size, i])
+        prefix.append(level[0, i])
     state = jnp.zeros((DK, DV), F32)
-    entry = state
     for i in range(groups - 1):
 
         @pl.when(team > i)
@@ -225,35 +299,42 @@
             remote(total_got.at[i], total_got.at[i], s2.at[0], r2.at[i], {"seq": mates[0]}).wait_recv()
 
         whole = total_got[i].astype(F32)
-        moved = state + whole[:, DK:] - mm(whole[:, :DK].astype(BF16), state.astype(BF16))
+        moved = whole[:, DK:]
+        if i > 0:
+            moved = moved + state - mm(whole[:, :DK].astype(BF16), state.astype(BF16))
         state = jnp.where(team > i, moved, state)
     entry = state
     rounded = entry.astype(BF16)
-    for i in range(members):
-        begin = entry
-        if i > 0:
-            begin = entry + prefix[i][:, DK:] - mm(prefix[i][:, :DK].astype(BF16), rounded)
+    start[0] = rounded
+    for i in range(1, members):
+        begin = entry + prefix[i][:, DK:] - mm(prefix[i][:, :DK].astype(BF16), rounded)
         start[i] = begin.astype(BF16)
-    for d in range(1, members):
-        to = lax.rem(slot + d, members)
+    turns = [(n * members // 4, c) for n in (0, 1, 3, 2) for c in range(members // 4)]
+    near = [
+        lax.rem(slot - lax.rem(slot, members // 4) + n, members) + lax.rem(slot + c, members // 4)
+        for n, c in turns
+    ]
+    for d in reversed(range(1, members)):
         copy = remote(
-            start.at[to], state_ref.at[slot], s3.at[d], r3.at[slot], {"seq": peers[d - 1]}
+            start.at[near[d]],
+            state_ref.at[slot],
+            s3.at[d],
+            r3.at[slot],
+            {"seq": team * members + near[d]},
         )
         copy.start()
         sends.append(copy)
     state_ref[slot] = start[slot]
-    for i in range(members):
-
-        @pl.when(slot != i)
-        def _():
+    for d in range(members):
+        i = near[d]
+        if d > 0:
             remote(state_ref.at[i], state_ref.at[i], s3.at[0], r3.at[i], {"seq": peers[0]}).wait_recv()
-
-        at = slice(i * DV, (i + 1) * DV)
+        at = pl.ds(pl.multiple_of(i * DV, DV), DV)
         attended = part_ref[:, at] + mm(ask_ref[:, at], state_ref[i])
         scale = lax.rsqrt(jnp.mean(attended * attended, axis=-1, keepdims=True) + eps_norm)
         gated_ref[:, at] = (attended * scale * gate_ref[:, at]).astype(BF16)
 
-    loads[5].wait()
+    load_o.wait()
     gated = gated_ref[...]
     tile = out_ref.shape[1]
     half = rows // 2
@@ -297,6 +378,12 @@
         ).astype(BF16)
 
     edge.wait_send()
+    for j in range(members):
+
+        @pl.when(slot != j)
+        def _():
+            carry_copy(j).wait_send()
+
     for copy in sends + hops + lands + ends:
         copy.wait_send()
     for d in range(1, groups):
@@ -332,9 +419,11 @@
     like = lambda a: pltpu.VMEM(a.shape, a.dtype)
     dma = pltpu.SemaphoreType.DMA
     bufs = [like(a) for a in (hidden, w_query, w_key, w_value, w_gate, w_out)]
-    bufs += [pltpu.VMEM((HALO, depth), BF16), dma((6,)), dma, dma]
+    bufs += [pltpu.VMEM((HALO, depth), BF16), dma((5 + VALUE_PARTS,)), dma, dma]
     rule = [
-        pltpu.VMEM((rows + 8, wide), F32),
+        pltpu.VMEM((rows + 8, wide // VALUE_PARTS), F32),
+        pltpu.VMEM((rows + 8, w_key.shape[1]), F32),
+        pltpu.VMEM((rows + 8, w_query.shape[1]), F32),
         pltpu.VMEM((rows, wide), F32),
         pltpu.VMEM((rows, wide), BF16),
         pltpu.VMEM((heads, DK, DK + DV), BF16),

time: 50.6 us -> 48.3 us (0.955)
  Pallas kernels: 48.7 us -> 46.4 us
    pallas_call x1, Pallas kernels: 48.7 us -> 46.4 us  [shards(): pl.pallas_call(functools.partial(layer_kernel, (size_seq, size_head, head...]
where the time goes in v3:
time: 48.3 us; the launch traced here: 48.1 us
  Pallas kernels  46.4 us (96%)
  local copies, waits for them, and re-layouts  1.67 us (3%)
    pallas_call x1, Pallas kernels, shards(): pl.pallas_call(functools.partial(layer_kernel, (size_seq, size_head, head...  46.4 us
    unnamed x1, local copies, waits for them, and re-layouts  1.67 us

profile of v3, /device:TPU:64, one launch (start us, length us, event | category | flops | bytes accessed | tf_op | source)
XLA Modules:
  0.0 48.1 jit_solution(14530001439300071507)
XLA Ops:
  0.0 46.4 %layer.1 = bf16[256,512]{1,0:T(8,128)(2,1)} custom-call(bf16[256,2048]{1,0:T(8,128)(2,1)} %hid.1, bf16[2048,512]{1,0:T(8,128)(2,1)} %wq.1, bf16[2048,512]{1,0:T(8,128)(2,1)} %wk.1, bf16[2048,1024]{1,0:T(8,128)(2,1)} %wv.1, bf16[2048,1024]{1,0:T(8,128)(2,1)} %wg.1, bf16[8,2048]{1,0:T(8,128)(2,1)} %bitcast.2, bf16[4,512]{1,0:T(4,128)(2,1)} %cq.1, ...), custom_call_target="tpu_custom_call" | custom-call | tf_op jit(solution)/shard_map/layer/pallas_call | solution.py:442
  46.4 1.7 %copy.13 = bf16[256,512]{1,0:T(8,128)(2,1)} copy(bf16[256,512]{1,0:T(8,128)(2,1)} %layer.1) | data formatting | bytes 524288

commit v4 on v3

--- a/solution.py
+++ b/solution.py
@@ -11,7 +11,6 @@
 DV = 128
 KER = 4
 HALO = 16
-VALUE_PARTS = 2
 eps_norm = 1e-06
 F32 = jnp.float32
 BF16 = jnp.bfloat16
@@ -43,7 +42,7 @@
     return x * lax.rsqrt(jnp.sum(x * x, axis=-1, keepdims=True) + eps_norm)
 
 
-def block_solve(systems):
+def block_solve(systems, fill):
     n = systems[0].shape[0]
     row = lax.broadcasted_iota(jnp.int32, (n, n), 0)
     col = lax.broadcasted_iota(jnp.int32, (n, n), 1)
@@ -66,6 +65,7 @@
     powers = [-pick(a, size, 0, 1) for a in systems]
     solved = [eye + p for p in powers]
     powers = [mm(p.astype(BF16), spread(p, size, same)) for p in powers]
+    fill()
     for last in (False, False, True):
         wide = [spread(p, size, same) for p in powers]
         if last:
@@ -77,6 +77,7 @@
             ]
             solved = [x + y[:size] for x, y in zip(solved, both)]
             powers = [y[size:] for y in both]
+        fill()
     while size < n:
         same = (row // size) == (col // size)
         below = ((row // size) == (col // size) + 1) & ((row // size) % 2 == 1)
@@ -85,24 +86,23 @@
             mm(pick(a, size, 1, 2).astype(BF16), spread(x, size, same))
             for a, x in zip(systems, solved)
         ]
+        fill()
         cross = [mm(x.astype(BF16), spread(c, size, below)) for x, c in zip(solved, cross)]
         solved = [
             jnp.concatenate([jnp.where(odd, 0.0, x), jnp.where(odd, x, -c)], axis=0)
             for x, c in zip(solved, cross)
         ]
         size *= 2
+        fill()
     return [x.astype(BF16) for x in solved]
 
 
-def key_side(queries, keys, betas):
-    rows = keys[0].shape[0]
-    half = rows // 2
+def key_side(keys, betas, fill):
+    half = keys[0].shape[0] // 2
     row = lax.broadcasted_iota(jnp.int32, (half, half), 0)
     col = lax.broadcasted_iota(jnp.int32, (half, half), 1)
-    qb = [q.astype(BF16) for q in queries]
     kb = [k.astype(BF16) for k in keys]
     grams = [mm_nt(k, k) for k in kb]
-    scores = [mm_nt(q, k) for q, k in zip(qb, kb)]
     systems, corners = [], []
     for gram, many in zip(grams, betas):
         first = jnp.where(row > col, gram[:half, :half], 0.0)
@@ -110,20 +110,27 @@
         for b in many:
             systems += [b[:half] * first, b[half:] * last]
             corners.append((b[half:] * gram[half:, :half]).astype(BF16))
-    inverses = block_solve(systems)
+    inverses = block_solve(systems, fill)
+    return kb, list(zip(inverses[::2], inverses[1::2], corners))
+
+
+def query_side(queries, kb):
+    half = queries[0].shape[0] // 2
+    row = lax.broadcasted_iota(jnp.int32, (half, half), 0)
+    col = lax.broadcasted_iota(jnp.int32, (half, half), 1)
     masked = []
-    for score in scores:
+    for q, k in zip(queries, kb):
+        score = mm_nt(q.astype(BF16), k)
         upper = jnp.where(row >= col, score[:half, :half], 0.0).astype(BF16)
         lower = jnp.concatenate(
             [score[half:, :half], jnp.where(row >= col, score[half:, half:], 0.0)], axis=1
         ).astype(BF16)
         masked.append((upper, lower))
-    return kb, masked, list(zip(inverses[::2], inverses[1::2], corners))
-
-
-def value_side(solves, keys, values, betas):
-    half = keys[0].shape[0] // 2
-    sides = [jnp.concatenate([b * k, b * v], axis=1) for k, v, b in zip(keys, values, betas)]
+    return masked
+
+
+def value_side(solves, sides):
+    half = sides[0].shape[0] // 2
     tops = [mm(x[0], s[:half].astype(BF16)).astype(BF16) for x, s in zip(solves, sides)]
     rest = [(s[half:] - mm(x[2], t)).astype(BF16) for s, x, t in zip(sides, solves, tops)]
     ends = [mm(x[1], r).astype(BF16) for x, r in zip(solves, rest)]
@@ -152,15 +159,10 @@
         )
 
     h_buf, q_buf, k_buf, v_buf, g_buf, o_buf, halo, load_sem, edge_send, edge_recv = bufs
-    rows, wide = h_buf.shape[0], v_buf.shape[1]
-    part_wide = wide // VALUE_PARTS
-    ways = [(hid, h_buf), (wk, k_buf), (wq, q_buf)]
-    for n in range(VALUE_PARTS):
-        at = pl.ds(n * part_wide, part_wide)
-        ways.append((wv.at[:, at], v_buf.at[:, at]))
-    ways += [(wg, g_buf), (wo, o_buf)]
+    rows = h_buf.shape[0]
+    ways = ((hid, h_buf), (wk, k_buf), (wq, q_buf), (wv, v_buf), (wg, g_buf), (wo, o_buf))
     loads = [pltpu.make_async_copy(src, dst, load_sem.at[i]) for i, (src, dst) in enumerate(ways)]
-    load_h, load_k, load_q, *load_v, load_g, load_o = loads
+    load_h, load_k, load_q, load_v, load_g, load_o = loads
     for copy in loads[:-2]:
         copy.start()
 
@@ -174,7 +176,7 @@
     edge = remote(hid.at[pl.ds(rows - HALO, HALO)], halo, edge_send, edge_recv, {"seq": after})
     edge.start()
 
-    ext_ref, ext_k, ext_q, part_ref, ask_ref, carry_ref = rule
+    ext_v, ext_k, ext_q, part_ref, ask_ref, carry_ref = rule
     load_h.wait()
     h = h_buf[...]
     beta = 0.05 + 0.15 * sigmoid(mm_nt(h, wb[...]))
@@ -183,31 +185,43 @@
         jnp.sum(jnp.where(lane == j, beta, 0.0), axis=1, keepdims=True)
         for j in range(beta.shape[1])
     ]
-    def convolve(ext, taps, width):
-        t = 0.5 * taps.astype(F32)
-        summed = t[:1] * ext[pl.ds(8 - KER + 1, rows), :width]
-        for j in range(1, KER):
-            summed = summed + t[j : j + 1] * ext[pl.ds(8 - KER + 1 + j, rows), :width]
-        x = summed + summed * jnp.tanh(summed)
-        return [x[:, j * DK : (j + 1) * DK] for j in range(width // DK)]
-
-    load_k.wait()
-    ext_k[8:] = mm(h, k_buf[...])
-    load_q.wait()
-    ext_q[8:] = mm(h, q_buf[...])
+    def convolve(ext, taps, j):
+        at = slice(j * DK, (j + 1) * DK)
+        t = 0.5 * taps[:, at].astype(F32)
+        x = ext[:, at]
+        summed = t[KER - 1 :] * x
+        for n in range(KER - 1):
+            summed = summed + t[n : n + 1] * pltpu.roll(x, KER - 1 - n, 0)
+        summed = summed[8:]
+        return summed + summed * jnp.tanh(summed)
+
+    projections = ((load_k, k_buf, ext_k), (load_q, q_buf, ext_q), (load_v, v_buf, ext_v))
+    for load, w, ext in projections:
+        load.wait()
+        ext[8:] = mm(h, w[...])
+    load_g.start()
+    load_o.start()
     edge.wait_recv()
     border = halo[...]
     border = jnp.where(me > 0, border, jnp.zeros_like(border))
-    tall = jnp.concatenate([border, h], axis=0)
-    ext_k[:8] = mm(border, k_buf[...])[HALO - 8 :]
-    ext_q[:8] = mm(border, q_buf[...])[HALO - 8 :]
-    keys = [unit_rows(x) for x in convolve(ext_k, ck[...], k_buf.shape[1])]
-    queries = [unit_rows(x) for x in convolve(ext_q, cq[...], q_buf.shape[1])]
+    for _, w, ext in projections:
+        ext[:8] = mm(border, w[...])[HALO - 8 :]
     heads = len(betas)
-    group = heads // len(keys)
-    kb, masked, solves = key_side(
-        queries, keys, [betas[j : j + group] for j in range(0, heads, group)]
-    )
+    count = k_buf.shape[1] // DK
+    group = heads // count
+    keys = [unit_rows(convolve(ext_k, ck, j)) for j in range(count)]
+    sides = []
+
+    def fill():
+        j = len(sides)
+        if j < heads:
+            b = betas[j]
+            v = convolve(ext_v, cv, j)
+            sides.append(jnp.concatenate([b * keys[j // group], b * v], axis=1))
+
+    kb, solves = key_side(keys, [betas[j : j + group] for j in range(0, heads, group)], fill)
+    while len(sides) < heads:
+        fill()
 
     got, total, total_got, start, state_ref, s1, r1, s2, r2, s3, r3 = scan
 
@@ -216,37 +230,20 @@
             carry_ref.at[j], got.at[slot], s1.at[j], r1.at[slot], {"seq": team * members + j}
         )
 
-    sides = []
-    per = heads // VALUE_PARTS
-    for n in range(VALUE_PARTS):
-        load_v[n].wait()
-        if n == VALUE_PARTS - 1:
-            load_g.start()
-            load_o.start()
-        at = pl.ds(n * part_wide, part_wide)
-        ext_ref[...] = mm(tall, v_buf[:, at])[HALO - 8 :]
-        values = convolve(ext_ref, cv[:, at], part_wide)
-        mine = range(n * per, (n + 1) * per)
-        some = value_side(
-            [solves[j] for j in mine],
-            [keys[j // group] for j in mine],
-            values,
-            [betas[j] for j in mine],
-        )
-        for j, side in zip(mine, some):
-            carry_ref[j] = mm_tn(kb[j // group], side).astype(BF16)
-
-            @pl.when(slot != j)
-            def _():
-                carry_copy(j).start()
-
-            @pl.when(slot == j)
-            def _():
-                got[j] = carry_ref[j]
-
-        sides += some
+    sides = value_side(solves, sides)
+    for j, side in enumerate(sides):
+        carry_ref[j] = mm_tn(kb[j // group], side).astype(BF16)
+    for j in range(heads):
+
+        @pl.when(slot != j)
+        def _():
+            carry_copy(j).start()
+
+    got[slot] = carry_ref[slot]
 
     half = rows // 2
+    queries = [unit_rows(convolve(ext_q, cq, j)) for j in range(count)]
+    masked = query_side(queries, kb)
     for j, side in enumerate(sides):
         at = slice(j * DV, (j + 1) * DV)
         upper, lower = masked[j // group]
@@ -325,14 +322,14 @@
         copy.start()
         sends.append(copy)
     state_ref[slot] = start[slot]
-    for d in range(members):
-        i = near[d]
-        if d > 0:
+    for d in range(0, members, 2):
+        for i in near[max(d, 1) : d + 2]:
             remote(state_ref.at[i], state_ref.at[i], s3.at[0], r3.at[i], {"seq": peers[0]}).wait_recv()
-        at = pl.ds(pl.multiple_of(i * DV, DV), DV)
-        attended = part_ref[:, at] + mm(ask_ref[:, at], state_ref[i])
-        scale = lax.rsqrt(jnp.mean(attended * attended, axis=-1, keepdims=True) + eps_norm)
-        gated_ref[:, at] = (attended * scale * gate_ref[:, at]).astype(BF16)
+        at = [pl.ds(pl.multiple_of(i * DV, DV), DV) for i in near[d : d + 2]]
+        pair = [part_ref[:, c] + mm(ask_ref[:, c], state_ref[i]) for c, i in zip(at, near[d : d + 2])]
+        scales = [lax.rsqrt(jnp.mean(x * x, axis=-1, keepdims=True) + eps_norm) for x in pair]
+        for c, x, scale in zip(at, pair, scales):
+            gated_ref[:, c] = (x * scale * gate_ref[:, c]).astype(BF16)
 
     load_o.wait()
     gated = gated_ref[...]
@@ -419,9 +416,9 @@
     like = lambda a: pltpu.VMEM(a.shape, a.dtype)
     dma = pltpu.SemaphoreType.DMA
     bufs = [like(a) for a in (hidden, w_query, w_key, w_value, w_gate, w_out)]
-    bufs += [pltpu.VMEM((HALO, depth), BF16), dma((5 + VALUE_PARTS,)), dma, dma]
+    bufs += [pltpu.VMEM((HALO, depth), BF16), dma((6,)), dma, dma]
     rule = [
-        pltpu.VMEM((rows + 8, wide // VALUE_PARTS), F32),
+        pltpu.VMEM((rows + 8, wide), F32),
         pltpu.VMEM((rows + 8, w_key.shape[1]), F32),
         pltpu.VMEM((rows + 8, w_query.shape[1]), F32),
         pltpu.VMEM((rows, wide), F32),
@@ -443,7 +440,7 @@
         functools.partial(layer_kernel, (size_seq, size_head, heads)),
         in_specs=[hbm] * 5 + [vmem] * 5 + [hbm],
         out_specs=vmem,
-        out_shape=jax.ShapeDtypeStruct((rows, tile), BF16),
+        out_shape=pltpu.VMEM((rows, tile), BF16),
         scratch_shapes=[bufs, rule, scan, shares],
         compiler_params=pltpu.CompilerParams(collective_id=0, has_side_effects=True),
         name="layer",

time: 48.3 us -> 45.7 us (0.946)
  Pallas kernels: 46.4 us -> 44.8 us
  local copies, waits for them, and re-layouts: 1.67 us -> 0.71 us
    pallas_call x1, Pallas kernels: 46.4 us -> 44.8 us  [shards(): pl.pallas_call(functools.partial(layer_kernel, (size_seq, size_head, head...]
    unnamed x1, local copies, waits for them, and re-layouts: 1.67 us -> 0.71 us
where the time goes in v4:
time: 45.7 us; the launch traced here: 45.5 us
  Pallas kernels  44.8 us (98%)
  local copies, waits for them, and re-layouts  0.71 us (2%)
    pallas_call x1, Pallas kernels, shards(): pl.pallas_call(functools.partial(layer_kernel, (size_seq, size_head, head...  44.8 us

profile of v4, /device:TPU:64, one launch (start us, length us, event | category | flops | bytes accessed | tf_op | source)
XLA Modules:
  0.0 45.5 jit_solution(3167174104567703226)
XLA Ops:
  0.0 44.8 %layer.1 = bf16[256,512]{1,0:T(8,128)(2,1)S(1)} custom-call(bf16[256,2048]{1,0:T(8,128)(2,1)} %hid.1, bf16[2048,512]{1,0:T(8,128)(2,1)} %wq.1, bf16[2048,512]{1,0:T(8,128)(2,1)} %wk.1, bf16[2048,1024]{1,0:T(8,128)(2,1)} %wv.1, bf16[2048,1024]{1,0:T(8,128)(2,1)} %wg.1, bf16[8,2048]{1,0:T(8,128)(2,1)} %bitcast.2, bf16[4,512]{1,0:T(4,128)(2,1)} %cq.1, ...), custom_call_target="tpu_custom_call" | custom-call | tf_op jit(solution)/shard_map/layer/pallas_call | solution.py:439
  44.8 0.7 %copy.13 = bf16[256,512]{1,0:T(8,128)(2,1)} copy(bf16[256,512]{1,0:T(8,128)(2,1)S(1)} %layer.1) | data formatting | bytes 524288
